TPU v7x, 32 devices: a whole 2x2x4 slice. The times are simulated.
32 devices in a mesh: ctx: 16 (over z, y, core), fsdp: 2 (over x).
Axes of the slice: x: 2, y: 2, z: 4, core: 2. Of those that a mesh axis runs over, the one named last changes fastest.
Arguments:
- outer_gate: bfloat16 [8192, 2048], P('ctx', 'fsdp'), may hold values from -6 to 6
- inner_gate: bfloat16 [8192, 2048], P('ctx', 'fsdp'), may hold values from -6 to 6
- values: bfloat16 [8192, 2048], P('ctx', 'fsdp'), may hold values from -6 to 6
- out_weight: bfloat16 [2048, 2048], P('ctx', 'fsdp'), may hold values from -0.125 to 0.125
- skip_gain: float32 [2048], P('fsdp'), may hold values from 0.25 to 1.5
- residues: float32 [2048, 16], P('fsdp')
- decay_rates: float32 [2048, 16], P('fsdp')
- out_grad: bfloat16 [8192, 2048], P('ctx', 'fsdp'), may hold values from -6 to 6
Outputs:
- block_out: bfloat16 [8192, 2048], P('ctx', 'fsdp')
- outer_grad: bfloat16 [8192, 2048], P('ctx', 'fsdp')
- inner_grad: bfloat16 [8192, 2048], P('ctx', 'fsdp')
- value_grad: bfloat16 [8192, 2048], P('ctx', 'fsdp')
- weight_grad: float32 [2048, 2048], P('ctx', 'fsdp')
All inputs are finite; a program needn't handle non-finite values.
Results may differ from a plain program's by a relative error of at most 0.011.
Values may be sent and summed in bfloat16 or wider, within the bound.
A program may use at most 192 MiB of HBM per device.

v0:
```python
import math

import jax
import jax.numpy as jnp
from jax import lax
from jax.sharding import PartitionSpec as P


def passed_along(block, axis, distance):
    devices = range(lax.axis_size(axis))
    route = [(i - distance, i) for i in devices if i - distance in devices]
    return lax.ppermute(block, axis, route)


def mode_tables(residues, decay_rates, row_count):
    block_rows = min(64, row_count)
    lag_steps = jnp.arange(block_rows, dtype=jnp.float32)
    lag_index = jnp.arange(block_rows)[:, None] - jnp.arange(block_rows)[None, :]
    kernel = jnp.sum(
        residues[:, :, None] * jnp.exp(-decay_rates[:, :, None] * lag_steps[None, None, :]), axis=1
    )
    picked = kernel[:, jnp.clip(lag_index, 0, block_rows - 1)]
    toeplitz = jnp.where((lag_index >= 0)[None], picked, jnp.zeros_like(picked))
    rise_table = jnp.exp(-decay_rates[None] * (lag_steps[:, None, None] + 1.0))
    tail_table = jnp.exp(-decay_rates[None] * (block_rows - 1.0 - lag_steps)[:, None, None])
    return (block_rows, toeplitz, rise_table, tail_table)


def local_forward(inputs, decay_rates, tables):
    block_rows, toeplitz, rise_table, tail_table = tables
    blocks = inputs.shape[0] // block_rows
    shaped = inputs.reshape(blocks, block_rows, inputs.shape[1])
    inner_part = jnp.einsum("cts,nsc->ntc", toeplitz, shaped, precision=lax.Precision.HIGHEST)
    end_terms = jnp.einsum("nsc,scr->ncr", shaped, tail_table, precision=lax.Precision.HIGHEST)
    step_decay = jnp.exp(-decay_rates * block_rows)

    def advance(running, end_term):
        return (step_decay * running + end_term, running)

    end_state, befores = lax.scan(advance, jnp.zeros(decay_rates.shape, jnp.float32), end_terms)
    return (inner_part, befores, end_state)


def finish_forward(inner_part, befores, incoming, residues, decay_rates, tables):
    block_rows, toeplitz, rise_table, tail_table = tables
    blocks = inner_part.shape[0]
    offsets = block_rows * jnp.arange(blocks, dtype=jnp.float32)
    powers = jnp.exp(-decay_rates[None] * offsets[:, None, None])
    states = befores + powers * incoming[None]
    cross_part = jnp.einsum(
        "tcr,ncr->ntc", rise_table * residues[None], states, precision=lax.Precision.HIGHEST
    )
    total = inner_part + cross_part
    return total.reshape(blocks * block_rows, total.shape[2])


def local_backward(grads, decay_rates, tables):
    block_rows, toeplitz, rise_table, tail_table = tables
    blocks = grads.shape[0] // block_rows
    shaped = grads.reshape(blocks, block_rows, grads.shape[1])
    inner_part = jnp.einsum("cts,ntc->nsc", toeplitz, shaped, precision=lax.Precision.HIGHEST)
    start_terms = jnp.einsum("ntc,tcr->ncr", shaped, rise_table, precision=lax.Precision.HIGHEST)
    step_decay = jnp.exp(-decay_rates * block_rows)

    def retreat(running, start_term):
        return (step_decay * running + start_term, running)

    start_state, afters = lax.scan(
        retreat, jnp.zeros(decay_rates.shape, jnp.float32), start_terms, reverse=True
    )
    return (inner_part, afters, start_state)


def finish_backward(inner_part, afters, outgoing, residues, decay_rates, tables):
    block_rows, toeplitz, rise_table, tail_table = tables
    blocks = inner_part.shape[0]
    offsets = block_rows * (blocks - 1.0 - jnp.arange(blocks, dtype=jnp.float32))
    powers = jnp.exp(-decay_rates[None] * offsets[:, None, None])
    states = afters + powers * outgoing[None]
    cross_part = jnp.einsum(
        "scr,ncr->nsc", tail_table * residues[None], states, precision=lax.Precision.HIGHEST
    )
    total = inner_part + cross_part
    return total.reshape(blocks * block_rows, total.shape[2])


def shards(outer_gate, inner_gate, values, out_weight, skip_gain, residues, decay_rates, out_grad):
    row_count, channels = values.shape
    panel_full = lax.all_gather(out_weight, "ctx", axis=0, tiled=True)
    tables = mode_tables(residues, decay_rates, row_count)
    whole_decay = jnp.exp(-decay_rates * row_count)
    zero_state = jnp.zeros(decay_rates.shape, jnp.float32)
    gated = inner_gate.astype(jnp.float32) * values.astype(jnp.float32)
    inner_part, befores, local_end = local_forward(gated, decay_rates, tables)

    def relay_step(step_index, running):
        ending, received = running
        received = passed_along(ending, "ctx", 1)
        return (whole_decay * received + local_end, received)

    incoming = lax.fori_loop(0, lax.axis_size("ctx") - 1, relay_step, (local_end, zero_state))[1]
    filtered = (
        finish_forward(inner_part, befores, incoming, residues, decay_rates, tables)
        + skip_gain[None] * gated
    )
    modulated = (outer_gate.astype(jnp.float32) * filtered).astype(jnp.bfloat16)
    shard_piece = lax.all_gather(modulated, "fsdp", axis=1, tiled=True)
    out_total = jnp.dot(shard_piece, panel_full, preferred_element_type=jnp.float32)
    grad_rows = lax.dot_general(
        shard_piece, out_grad, (((0,), (0,)), ((), ())), preferred_element_type=jnp.float32
    )
    block_out = out_total.astype(jnp.bfloat16)
    partial_term = jnp.dot(out_grad, panel_full.T, preferred_element_type=jnp.float32)
    modulated_grad = lax.psum_scatter(
        partial_term.astype(jnp.bfloat16), "fsdp", scatter_dimension=1, tiled=True
    ).astype(jnp.float32)
    outer_grad = (modulated_grad * filtered).astype(jnp.bfloat16)
    filtered_grad = modulated_grad * outer_gate.astype(jnp.float32)
    inner_back, afters, local_start = local_backward(filtered_grad, decay_rates, tables)

    def return_step(step_index, running):
        ending, received = running
        received = passed_along(ending, "ctx", -1)
        return (whole_decay * received + local_start, received)

    outgoing = lax.fori_loop(0, lax.axis_size("ctx") - 1, return_step, (local_start, zero_state))[1]
    gated_grad = (
        finish_backward(inner_back, afters, outgoing, residues, decay_rates, tables)
        + skip_gain[None] * filtered_grad
    )
    inner_grad = (gated_grad * values.astype(jnp.float32)).astype(jnp.bfloat16)
    value_grad = (gated_grad * inner_gate.astype(jnp.float32)).astype(jnp.bfloat16)
    grad_scale = 1.0 / math.sqrt(row_count * lax.axis_size("ctx"))
    weight_grad = lax.psum_scatter(grad_rows, "ctx", scatter_dimension=0, tiled=True) * grad_scale
    return (block_out, outer_grad, inner_grad, value_grad, weight_grad)


def solution(mesh):
    placed = (
        P("ctx", "fsdp"),
        P("ctx", "fsdp"),
        P("ctx", "fsdp"),
        P("ctx", "fsdp"),
        P("fsdp"),
        P("fsdp", None),
        P("fsdp", None),
        P("ctx", "fsdp"),
    )
    return jax.shard_map(
        shards,
        mesh=mesh,
        in_specs=placed,
        out_specs=(
            P("ctx", "fsdp"),
            P("ctx", "fsdp"),
            P("ctx", "fsdp"),
            P("ctx", "fsdp"),
            P("ctx", "fsdp"),
        ),
        check_vma=False,
    )
```

profile of v0, /device:TPU:0, one launch (start us, length us, event | category | flops | bytes accessed | tf_op | source)
XLA Modules:
  0.0 623.6 jit_solution(16761147003697120696)
XLA Ops:
  8.0 1.9 convert_multiply_fusion.3
  9.9 2.8 copy.44
  14.7 1.6 multiply_reduce_fusion
  16.3 18.5 %gather_fusion = f32[4096,1024]{1,0:T(8,128)} fusion(f32[1024,64]{0,1:T(8,128)S(1)} %multiply_reduce_fusion, s32[4096]{0:T(1024)S(1)} %broadcast_clamp_fusion), kind=kCustom, calls=%fused_computation | custom fusion | bytes 33570816 | tf_op jit(solution)/shard_map/gather | solution.py:22
  34.8 30.5 %copy.43 = f32[64,64,1024]{1,0,2:T(8,128)} copy(f32[64,64,1024]{2,1,0:T(8,128)} %bitcast.64) | data formatting | bytes 33554432 | tf_op jit(solution)/shard_map/gather | solution.py:22
  65.4 17.3 %fusion.26 = f32[8,1024,16]{2,0,1:T(8,128)} fusion(f32[8,64,1024]{1,0,2:T(8,128)} %copy.44, f32[64]{0:T(128)S(1)} %iota_subtract_fusion, f32[1024,16]{1,0:T(8,128)S(1)} %copy.45), kind=kOutput, calls=%fused_computation.45 | convolution fusion | flops 101711872 | bytes 2687232 | tf_op jit(solution)/shard_map/nsc,scr->ncr/dot_general | solution.py:34
  82.6 3.2 copy.47
  85.9 5.8 convolution_convert_fusion
  92.5 57.3 %fusion.2 = f32[1024,8,64]{2,1,0:T(8,128)} fusion(f32[8,64,1024]{1,0,2:T(8,128)} %copy.44, f32[64,64,1024]{1,0,2:T(8,128)} %copy.43, pred[64,64]{1,0:T(8,128)(4,1)S(1)} %subtract_compare_fusion), kind=kOutput, calls=%fused_computation.9 | convolution fusion | flops 406847488 | bytes 20975616 | tf_op jit(solution)/shard_map/cts,nsc->ntc/dot_general | solution.py:33
  149.8 1.9 convert_multiply_fusion
  151.7 2.8 copy.51
  154.4 31.8 %fusion = f32[1024,8,64]{2,1,0:T(8,128)} fusion(f32[8,64,1024]{1,0,2:T(8,128)} %copy.51, f32[64,64,1024]{1,0,2:T(8,128)} %copy.43, pred[64,64]{1,0:T(8,128)(4,1)S(1)} %subtract_compare_fusion), kind=kOutput, calls=%fused_computation.7 | convolution fusion | flops 406847488 | bytes 20975616 | tf_op jit(solution)/shard_map/cts,ntc->nsc/dot_general | solution.py:61
  186.3 15.8 %fusion.27 = f32[8,1024,16]{2,0,1:T(8,128)} fusion(f32[8,64,1024]{1,0,2:T(8,128)S(1)} %copy-done.1, f32[64]{0:T(128)S(1)} %iota_add_fusion, f32[1024,16]{1,0:T(8,128)S(1)} %copy-done.5), kind=kOutput, calls=%fused_computation.46 | convolution fusion | flops 101711872 | bytes 2687232 | tf_op jit(solution)/shard_map/ntc,tcr->ncr/dot_general | solution.py:62
  202.1 2.9 copy.53
  206.2 97.3 %while.54 = (s32[]{:T(128)}, f32[1024,16]{0,1:T(8,128)S(1)}, f32[1024,16]{0,1:T(8,128)}, f32[1024,16]{0,1:T(8,128)S(1)}, f32[1024,16]{0,1:T(8,128)S(1)}, /*index=5*/s32[]{:T(128)}) while((s32[]{:T(128)}, f32[1024,16]{0,1:T(8,128)S(1)}, f32[1024,16]{0,1:T(8,128)}, f32[1024,16]{0,1:T(8,128)S(1)}, f32[1024,16]{0,1:T(8,128)S(1)}, ...), condition=%wide.region_4.5_spmd, body=%wide.region_3.4_spmd.sunk | while | flops 32770 | bytes 786569 | solution.py:101
  206.2 2.3 collective-permute-start
  210.1 4.9 collective-permute-start
  216.5 4.7 collective-permute-start
  222.8 4.7 collective-permute-start
  229.0 4.7 collective-permute-start
  235.2 4.7 collective-permute-start
  241.4 4.7 collective-permute-start
  247.6 4.8 collective-permute-start
  253.8 5.6 collective-permute-start
  260.9 5.6 collective-permute-start
  268.0 5.6 collective-permute-start
  275.1 5.6 collective-permute-start
  282.2 5.6 collective-permute-start
  289.3 5.6 collective-permute-start
  296.5 5.6 collective-permute-start
  304.2 107.5 %while.55 = (s32[]{:T(128)}, f32[1024,16]{0,1:T(8,128)S(1)}, f32[1024,16]{0,1:T(8,128)}, f32[1024,16]{0,1:T(8,128)S(1)}, f32[1024,16]{0,1:T(8,128)S(1)}, /*index=5*/s32[]{:T(128)}) while((s32[]{:T(128)}, f32[1024,16]{0,1:T(8,128)S(1)}, f32[1024,16]{0,1:T(8,128)}, f32[1024,16]{0,1:T(8,128)S(1)}, f32[1024,16]{0,1:T(8,128)S(1)}, ...), condition=%wide.region_9.10_spmd, body=%wide.region_8.9_spmd.sunk | while | flops 32770 | bytes 786569 | solution.py:126
  304.2 1.3 collective-permute-start.1
  305.5 5.0 collective-permute-done.1
  311.1 1.3 collective-permute-start.1
  312.4 5.8 collective-permute-done.1
  318.9 1.3 collective-permute-start.1
  320.2 5.0 collective-permute-done.1
  325.8 1.3 collective-permute-start.1
  327.1 5.8 collective-permute-done.1
  334.8 5.2 collective-permute-done.1
  341.9 5.2 collective-permute-done.1
  349.0 5.2 collective-permute-done.1
  356.2 5.2 collective-permute-done.1
  363.3 5.2 collective-permute-done.1
  370.4 5.2 collective-permute-done.1
  377.5 5.2 collective-permute-done.1
  384.6 5.2 collective-permute-done.1
  391.7 5.2 collective-permute-done.1
  398.8 5.2 collective-permute-done.1
  405.9 5.2 collective-permute-done.1
  411.7 1.9 multiply_add_fusion.2
  413.5 2.6 copy.49
  416.2 13.4 %add_bitcast_fusion.1 = f32[8,64,1024]{1,0,2:T(8,128)} fusion(f32[1024,8,64]{2,1,0:T(8,128)} %fusion.2, f32[8,1024,16]{2,0,1:T(8,128)} %copy.49, f32[1024,16]{1,0:T(8,128)} %copy.48, f32[64]{0:T(128)S(1)} %iota_add_fusion, f32[1024,16]{1,0:T(8,128)S(1)} %copy-done.5), kind=kOutput, calls=%fused_computation.26 | convolution fusion | flops 103284736 | bytes 4849920 | tf_op jit(solution)/shard_map/tcr,ncr->ntc/dot_general | solution.py:50
  429.6 2.8 copy.50
  432.4 3.6 copy.54
  436.0 13.8 %add_bitcast_fusion = f32[8,64,1024]{1,0,2:T(8,128)} fusion(f32[1024,8,64]{2,1,0:T(8,128)} %fusion, f32[8,1024,16]{2,0,1:T(8,128)} %copy.54, f32[1024,16]{1,0:T(8,128)} %copy.48, f32[64]{0:T(128)S(1)} %iota_subtract_fusion, f32[1024,16]{1,0:T(8,128)} %copy-done.4), kind=kOutput, calls=%fused_computation.25 | convolution fusion | flops 103284736 | bytes 4849920 | tf_op jit(solution)/shard_map/scr,ncr->nsc/dot_general | solution.py:80
  449.9 3.9 copy.55
  453.7 7.0 %fusion.35 = (bf16[512,1024]{1,0:T(8,128)(2,1)}, bf16[512,1024]{1,0:T(8,128)(2,1)}, bf16[512,1024]{1,0:T(8,128)(2,1)}, bf16[512,1024]{1,0:T(8,128)(2,1)}) fusion(bf16[512,1024]{1,0:T(8,128)(2,1)} %reduce-scatter.3.cloned.1.call-done, f32[1024]{0:T(1024)S(1)} %copy-done.13, f32[8,64,1024]{2,1,0:T(8,128)S(1)} %copy.50, bf16[512,1024]{1,0:T(8,128)(2,1)} %param.18, ...), kind=kLoop, calls=%fused_computation.50 | loop fusion | flops 9437184 | bytes 12587008 | tf_op jit(solution)/shard_map/convert_element_type | solution.py:117
  460.9 41.8 %all-gather.3.cloned.1.call-done = bf16[512,2048]{1,0:T(8,128)(2,1)} async-done(((bf16[512,1024]{1,0:T(8,128)(2,1)}), bf16[512,2048]{1,0:T(8,128)(2,1)}) %all-gather.3.cloned.1.call-update) | async-done | bytes 2097168 | tf_op jit(solution)/shard_map/all_gather | solution.py:107
  502.6 7.3 %fusion.38 = f32[2048,1024]{1,0:T(8,128)} fusion(bf16[512,2048]{1,0:T(8,128)(2,1)} %all-gather.3.cloned.1.call-done, bf16[512,1024]{1,0:T(8,128)(2,1)S(1)} %copy-done), kind=kOutput, calls=%fused_computation.68 | convolution fusion | flops 2147483648 | bytes 11534336 | tf_op jit(solution)/shard_map/dot_general | solution.py:109
  509.9 1.6 copy-done.14
  511.5 5.5 convolution_convert_fusion.1
  517.0 97.8 %reduce-scatter.5.cloned.1.call-done = f32[128,1024]{1,0:T(8,128)} async-done(((f32[2048,1024]{1,0:T(8,128)}), f32[128,1024]{1,0:T(8,128)}) %reduce-scatter.5.cloned.1.call-update) | async-done | bytes 524304 | tf_op jit(solution)/shard_map/reduce_scatter | solution.py:134
  614.7 1.9 broadcast_multiply_fusion
  (203 shorter events, 51.9 us)
Async XLA Ops:
  7.2 78.8 %copy-start = (bf16[512,1024]{1,0:T(8,128)(2,1)S(1)}, bf16[512,1024]{1,0:T(8,128)(2,1)}, u32[]{:S(2)}) copy-start(bf16[512,1024]{1,0:T(8,128)(2,1)} %param.23) | copy-start | bytes 3145732
  7.2 78.7 %all-gather.5.cloned.1.call-start = ((), (), s32[]{:S(2)}) async-start(), calls=%async_computation.3 | async-start | bytes 4456448 | tf_op jit(solution)/shard_map/all_gather | solution.py:89
  7.9 141.8 %reduce-scatter.3.cloned.1.call-start = ((), (), s32[]{:S(2)}) async-start(), calls=%async_computation.4 | async-start | bytes 3145728 | tf_op jit(solution)/shard_map/reduce_scatter | solution.py:114
  9.9 2.9 copy-start.12
  9.9 3.8 copy-start.11
  13.5 21.3 %copy-start.10 = (f32[1024,16]{0,1:T(8,128)}, f32[1024,16]{0,1:T(8,128)S(1)}, u32[]{:S(2)}) copy-start(f32[1024,16]{0,1:T(8,128)S(1)} %get-tuple-element.311) | copy-start | bytes 196612
  13.7 51.7 %copy-start.4 = (f32[1024,16]{1,0:T(8,128)}, f32[1024,16]{1,0:T(8,128)S(1)}, u32[]{:S(2)}) copy-start(f32[1024,16]{1,0:T(8,128)S(1)} %copy.45) | copy-start | bytes 196612
  91.8 410.8 %all-gather.3.cloned.1.call-start = ((), (), s32[]{:S(2)}) async-start(), calls=%async_computation.2 | async-start | bytes 3145728 | tf_op jit(solution)/shard_map/all_gather | solution.py:107
  92.4 57.3 %copy-start.8 = (f32[8,1024,16]{1,2,0:T(8,128)}, f32[8,1024,16]{1,2,0:T(8,128)S(1)}, u32[]{:S(2)}) copy-start(f32[8,1024,16]{1,2,0:T(8,128)S(1)} %get-tuple-element.189) | copy-start | bytes 1572868
  154.4 31.9 %copy-start.1 = (f32[8,64,1024]{1,0,2:T(8,128)S(1)}, f32[8,64,1024]{1,0,2:T(8,128)}, u32[]{:S(2)}) copy-start(f32[8,64,1024]{1,0,2:T(8,128)} %copy.51) | copy-start | bytes 6291460
  154.4 31.9 %copy-start.5 = (f32[1024,16]{1,0:T(8,128)S(1)}, f32[1024,16]{1,0:T(8,128)}, u32[]{:S(2)}) copy-start(f32[1024,16]{1,0:T(8,128)} %copy-done.4) | copy-start | bytes 196612
  202.1 2.9 copy-start.2
  202.1 4.1 copy-start.3
  202.1 209.6 %copy-start.9 = (f32[8,1024,16]{1,2,0:T(8,128)S(1)}, f32[8,1024,16]{1,2,0:T(8,128)}, u32[]{:S(2)}) copy-start(f32[8,1024,16]{1,2,0:T(8,128)} %copy-done.8) | copy-start | bytes 1572868
  206.2 3.2 collective-permute-start
  209.5 0.6 copy-start.7
  210.1 5.8 collective-permute-start
  215.9 0.6 copy-start.7
  216.5 5.6 collective-permute-start
  222.8 5.6 collective-permute-start
  229.0 5.6 collective-permute-start
  235.2 5.6 collective-permute-start
  241.4 5.6 collective-permute-start
  247.6 5.6 collective-permute-start
  253.8 6.5 %collective-permute-start = (f32[1024,16]{0,1:T(8,128)S(1)}, f32[1024,16]{0,1:T(8,128)S(1)}, u32[]{:S(2)}, u32[]{:S(2)}) collective-permute-start(f32[1024,16]{0,1:T(8,128)S(1)} %get-tuple-element.504), channel_id=1, source_target_pairs={{0,2},{2,4},{4,6},{6,8},{8,10},{10,12},{12,14},{14,16},{16,18},{18... | collective-permute-start | bytes 196616 | tf_op jit(solution)/shard_map/while/body/eval_jaxpr/ppermute | solution.py:12
  260.9 6.5 %collective-permute-start = (f32[1024,16]{0,1:T(8,128)S(1)}, f32[1024,16]{0,1:T(8,128)S(1)}, u32[]{:S(2)}, u32[]{:S(2)}) collective-permute-start(f32[1024,16]{0,1:T(8,128)S(1)} %get-tuple-element.504), channel_id=1, source_target_pairs={{0,2},{2,4},{4,6},{6,8},{8,10},{10,12},{12,14},{14,16},{16,18},{18... | collective-permute-start | bytes 196616 | tf_op jit(solution)/shard_map/while/body/eval_jaxpr/ppermute | solution.py:12
  268.0 6.5 %collective-permute-start = (f32[1024,16]{0,1:T(8,128)S(1)}, f32[1024,16]{0,1:T(8,128)S(1)}, u32[]{:S(2)}, u32[]{:S(2)}) collective-permute-start(f32[1024,16]{0,1:T(8,128)S(1)} %get-tuple-element.504), channel_id=1, source_target_pairs={{0,2},{2,4},{4,6},{6,8},{8,10},{10,12},{12,14},{14,16},{16,18},{18... | collective-permute-start | bytes 196616 | tf_op jit(solution)/shard_map/while/body/eval_jaxpr/ppermute | solution.py:12
  275.1 6.5 %collective-permute-start = (f32[1024,16]{0,1:T(8,128)S(1)}, f32[1024,16]{0,1:T(8,128)S(1)}, u32[]{:S(2)}, u32[]{:S(2)}) collective-permute-start(f32[1024,16]{0,1:T(8,128)S(1)} %get-tuple-element.504), channel_id=1, source_target_pairs={{0,2},{2,4},{4,6},{6,8},{8,10},{10,12},{12,14},{14,16},{16,18},{18... | collective-permute-start | bytes 196616 | tf_op jit(solution)/shard_map/while/body/eval_jaxpr/ppermute | solution.py:12
  282.2 6.5 %collective-permute-start = (f32[1024,16]{0,1:T(8,128)S(1)}, f32[1024,16]{0,1:T(8,128)S(1)}, u32[]{:S(2)}, u32[]{:S(2)}) collective-permute-start(f32[1024,16]{0,1:T(8,128)S(1)} %get-tuple-element.504), channel_id=1, source_target_pairs={{0,2},{2,4},{4,6},{6,8},{8,10},{10,12},{12,14},{14,16},{16,18},{18... | collective-permute-start | bytes 196616 | tf_op jit(solution)/shard_map/while/body/eval_jaxpr/ppermute | solution.py:12
  289.3 6.5 %collective-permute-start = (f32[1024,16]{0,1:T(8,128)S(1)}, f32[1024,16]{0,1:T(8,128)S(1)}, u32[]{:S(2)}, u32[]{:S(2)}) collective-permute-start(f32[1024,16]{0,1:T(8,128)S(1)} %get-tuple-element.504), channel_id=1, source_target_pairs={{0,2},{2,4},{4,6},{6,8},{8,10},{10,12},{12,14},{14,16},{16,18},{18... | collective-permute-start | bytes 196616 | tf_op jit(solution)/shard_map/while/body/eval_jaxpr/ppermute | solution.py:12
  296.5 6.5 %collective-permute-start = (f32[1024,16]{0,1:T(8,128)S(1)}, f32[1024,16]{0,1:T(8,128)S(1)}, u32[]{:S(2)}, u32[]{:S(2)}) collective-permute-start(f32[1024,16]{0,1:T(8,128)S(1)} %get-tuple-element.504), channel_id=1, source_target_pairs={{0,2},{2,4},{4,6},{6,8},{8,10},{10,12},{12,14},{14,16},{16,18},{18... | collective-permute-start | bytes 196616 | tf_op jit(solution)/shard_map/while/body/eval_jaxpr/ppermute | solution.py:12
  304.2 6.3 %collective-permute-start.1 = (f32[1024,16]{0,1:T(8,128)S(1)}, f32[1024,16]{0,1:T(8,128)S(1)}, u32[]{:S(2)}, u32[]{:S(2)}) collective-permute-start(f32[1024,16]{0,1:T(8,128)S(1)} %get-tuple-element.465), channel_id=1, source_target_pairs={{2,0},{4,2},{6,4},{8,6},{10,8},{12,10},{14,12},{16,14},{18,16},{20... | collective-permute-start | bytes 196616 | tf_op jit(solution)/shard_map/while/body/eval_jaxpr/ppermute | solution.py:12
  310.5 0.6 copy-start.6
  311.1 7.1 %collective-permute-start.1 = (f32[1024,16]{0,1:T(8,128)S(1)}, f32[1024,16]{0,1:T(8,128)S(1)}, u32[]{:S(2)}, u32[]{:S(2)}) collective-permute-start(f32[1024,16]{0,1:T(8,128)S(1)} %get-tuple-element.465), channel_id=1, source_target_pairs={{2,0},{4,2},{6,4},{8,6},{10,8},{12,10},{14,12},{16,14},{18,16},{20... | collective-permute-start | bytes 196616 | tf_op jit(solution)/shard_map/while/body/eval_jaxpr/ppermute | solution.py:12
  318.2 0.6 copy-start.6
  318.9 6.3 %collective-permute-start.1 = (f32[1024,16]{0,1:T(8,128)S(1)}, f32[1024,16]{0,1:T(8,128)S(1)}, u32[]{:S(2)}, u32[]{:S(2)}) collective-permute-start(f32[1024,16]{0,1:T(8,128)S(1)} %get-tuple-element.465), channel_id=1, source_target_pairs={{2,0},{4,2},{6,4},{8,6},{10,8},{12,10},{14,12},{16,14},{18,16},{20... | collective-permute-start | bytes 196616 | tf_op jit(solution)/shard_map/while/body/eval_jaxpr/ppermute | solution.py:12
  325.2 0.6 copy-start.6
  325.8 7.1 %collective-permute-start.1 = (f32[1024,16]{0,1:T(8,128)S(1)}, f32[1024,16]{0,1:T(8,128)S(1)}, u32[]{:S(2)}, u32[]{:S(2)}) collective-permute-start(f32[1024,16]{0,1:T(8,128)S(1)} %get-tuple-element.465), channel_id=1, source_target_pairs={{2,0},{4,2},{6,4},{8,6},{10,8},{12,10},{14,12},{16,14},{18,16},{20... | collective-permute-start | bytes 196616 | tf_op jit(solution)/shard_map/while/body/eval_jaxpr/ppermute | solution.py:12
  332.9 0.6 copy-start.6
  333.6 6.5 %collective-permute-start.1 = (f32[1024,16]{0,1:T(8,128)S(1)}, f32[1024,16]{0,1:T(8,128)S(1)}, u32[]{:S(2)}, u32[]{:S(2)}) collective-permute-start(f32[1024,16]{0,1:T(8,128)S(1)} %get-tuple-element.465), channel_id=1, source_target_pairs={{2,0},{4,2},{6,4},{8,6},{10,8},{12,10},{14,12},{16,14},{18,16},{20... | collective-permute-start | bytes 196616 | tf_op jit(solution)/shard_map/while/body/eval_jaxpr/ppermute | solution.py:12
  340.0 0.6 copy-start.6
  340.7 6.5 %collective-permute-start.1 = (f32[1024,16]{0,1:T(8,128)S(1)}, f32[1024,16]{0,1:T(8,128)S(1)}, u32[]{:S(2)}, u32[]{:S(2)}) collective-permute-start(f32[1024,16]{0,1:T(8,128)S(1)} %get-tuple-element.465), channel_id=1, source_target_pairs={{2,0},{4,2},{6,4},{8,6},{10,8},{12,10},{14,12},{16,14},{18,16},{20... | collective-permute-start | bytes 196616 | tf_op jit(solution)/shard_map/while/body/eval_jaxpr/ppermute | solution.py:12
  347.1 0.6 copy-start.6
  347.8 6.5 %collective-permute-start.1 = (f32[1024,16]{0,1:T(8,128)S(1)}, f32[1024,16]{0,1:T(8,128)S(1)}, u32[]{:S(2)}, u32[]{:S(2)}) collective-permute-start(f32[1024,16]{0,1:T(8,128)S(1)} %get-tuple-element.465), channel_id=1, source_target_pairs={{2,0},{4,2},{6,4},{8,6},{10,8},{12,10},{14,12},{16,14},{18,16},{20... | collective-permute-start | bytes 196616 | tf_op jit(solution)/shard_map/while/body/eval_jaxpr/ppermute | solution.py:12
  354.2 0.6 copy-start.6
  354.9 6.5 %collective-permute-start.1 = (f32[1024,16]{0,1:T(8,128)S(1)}, f32[1024,16]{0,1:T(8,128)S(1)}, u32[]{:S(2)}, u32[]{:S(2)}) collective-permute-start(f32[1024,16]{0,1:T(8,128)S(1)} %get-tuple-element.465), channel_id=1, source_target_pairs={{2,0},{4,2},{6,4},{8,6},{10,8},{12,10},{14,12},{16,14},{18,16},{20... | collective-permute-start | bytes 196616 | tf_op jit(solution)/shard_map/while/body/eval_jaxpr/ppermute | solution.py:12
  361.3 0.6 copy-start.6
  362.0 6.5 %collective-permute-start.1 = (f32[1024,16]{0,1:T(8,128)S(1)}, f32[1024,16]{0,1:T(8,128)S(1)}, u32[]{:S(2)}, u32[]{:S(2)}) collective-permute-start(f32[1024,16]{0,1:T(8,128)S(1)} %get-tuple-element.465), channel_id=1, source_target_pairs={{2,0},{4,2},{6,4},{8,6},{10,8},{12,10},{14,12},{16,14},{18,16},{20... | collective-permute-start | bytes 196616 | tf_op jit(solution)/shard_map/while/body/eval_jaxpr/ppermute | solution.py:12
  368.4 0.6 copy-start.6
  369.1 6.5 %collective-permute-start.1 = (f32[1024,16]{0,1:T(8,128)S(1)}, f32[1024,16]{0,1:T(8,128)S(1)}, u32[]{:S(2)}, u32[]{:S(2)}) collective-permute-start(f32[1024,16]{0,1:T(8,128)S(1)} %get-tuple-element.465), channel_id=1, source_target_pairs={{2,0},{4,2},{6,4},{8,6},{10,8},{12,10},{14,12},{16,14},{18,16},{20... | collective-permute-start | bytes 196616 | tf_op jit(solution)/shard_map/while/body/eval_jaxpr/ppermute | solution.py:12
  375.5 0.6 copy-start.6
  376.2 6.5 %collective-permute-start.1 = (f32[1024,16]{0,1:T(8,128)S(1)}, f32[1024,16]{0,1:T(8,128)S(1)}, u32[]{:S(2)}, u32[]{:S(2)}) collective-permute-start(f32[1024,16]{0,1:T(8,128)S(1)} %get-tuple-element.465), channel_id=1, source_target_pairs={{2,0},{4,2},{6,4},{8,6},{10,8},{12,10},{14,12},{16,14},{18,16},{20... | collective-permute-start | bytes 196616 | tf_op jit(solution)/shard_map/while/body/eval_jaxpr/ppermute | solution.py:12
  382.6 0.6 copy-start.6
  383.3 6.5 %collective-permute-start.1 = (f32[1024,16]{0,1:T(8,128)S(1)}, f32[1024,16]{0,1:T(8,128)S(1)}, u32[]{:S(2)}, u32[]{:S(2)}) collective-permute-start(f32[1024,16]{0,1:T(8,128)S(1)} %get-tuple-element.465), channel_id=1, source_target_pairs={{2,0},{4,2},{6,4},{8,6},{10,8},{12,10},{14,12},{16,14},{18,16},{20... | collective-permute-start | bytes 196616 | tf_op jit(solution)/shard_map/while/body/eval_jaxpr/ppermute | solution.py:12
  389.7 0.6 copy-start.6
  390.4 6.5 %collective-permute-start.1 = (f32[1024,16]{0,1:T(8,128)S(1)}, f32[1024,16]{0,1:T(8,128)S(1)}, u32[]{:S(2)}, u32[]{:S(2)}) collective-permute-start(f32[1024,16]{0,1:T(8,128)S(1)} %get-tuple-element.465), channel_id=1, source_target_pairs={{2,0},{4,2},{6,4},{8,6},{10,8},{12,10},{14,12},{16,14},{18,16},{20... | collective-permute-start | bytes 196616 | tf_op jit(solution)/shard_map/while/body/eval_jaxpr/ppermute | solution.py:12
  396.8 0.6 copy-start.6
  397.5 6.5 %collective-permute-start.1 = (f32[1024,16]{0,1:T(8,128)S(1)}, f32[1024,16]{0,1:T(8,128)S(1)}, u32[]{:S(2)}, u32[]{:S(2)}) collective-permute-start(f32[1024,16]{0,1:T(8,128)S(1)} %get-tuple-element.465), channel_id=1, source_target_pairs={{2,0},{4,2},{6,4},{8,6},{10,8},{12,10},{14,12},{16,14},{18,16},{20... | collective-permute-start | bytes 196616 | tf_op jit(solution)/shard_map/while/body/eval_jaxpr/ppermute | solution.py:12
  403.9 0.6 copy-start.6
  404.6 6.5 %collective-permute-start.1 = (f32[1024,16]{0,1:T(8,128)S(1)}, f32[1024,16]{0,1:T(8,128)S(1)}, u32[]{:S(2)}, u32[]{:S(2)}) collective-permute-start(f32[1024,16]{0,1:T(8,128)S(1)} %get-tuple-element.465), channel_id=1, source_target_pairs={{2,0},{4,2},{6,4},{8,6},{10,8},{12,10},{14,12},{16,14},{18,16},{20... | collective-permute-start | bytes 196616 | tf_op jit(solution)/shard_map/while/body/eval_jaxpr/ppermute | solution.py:12
  411.0 0.6 copy-start.6
  449.9 3.9 copy-start.13
  460.8 153.9 %reduce-scatter.5.cloned.1.call-start = ((), (), s32[]{:S(2)}) async-start(), calls=%async_computation.5 | async-start | bytes 8912896 | tf_op jit(solution)/shard_map/reduce_scatter | solution.py:134
  509.9 1.6 copy-start.14
  (13 other events, 8.2 us)
Sparse Core Ops, SparseCore 0:
  10.2 53.2 all-gather.4
  91.9 34.4 reduce-scatter.2
  460.9 41.6 all-gather.2
  510.0 104.6 reduce-scatter.4
where the time goes:
time: 633 us; the launch traced here: 624 us
  waiting for transfers between devices  232 us (37%)
  matrix products  168 us (27%)
  local copies, waits for them, and re-layouts  96.3 us (15%)
  starting transfers between devices  93.9 us (15%)
  other arithmetic  17.8 us (3%)
  between operations  14.4 us (2%)
    reduce_scatter x1, waiting for transfers between devices, shards(): lax.psum_scatter(grad_rows, 'ctx', scatter_dimension=0, tiled=True)  97.8 us
    ppermute x30, starting transfers between devices, passed_along(): return lax.ppermute(block, axis, route)  93.7 us
    ppermute x30, waiting for transfers between devices, passed_along(): return lax.ppermute(block, axis, route)  91.9 us
    dot_general x1, matrix products, local_forward(): jnp.einsum('cts,nsc->ntc', toeplitz, shaped, precision=lax.Precision.HIGH...  57.3 us
    gather x2, local copies, waits for them, and re-layouts, mode_tables(): picked = kernel[:, jnp.clip(lag_index, 0, block_rows - 1)]  49.1 us
    all_gather x1, waiting for transfers between devices, shards(): shard_piece = lax.all_gather(modulated, 'fsdp', axis=1, tiled=True)  41.8 us
    dot_general x1, matrix products, local_backward(): jnp.einsum('cts,ntc->nsc', toeplitz, shaped, precision=lax.Precision.HIGH...  31.8 us
    while x60, local copies, waits for them, and re-layouts  18.4 us
  transfers between devices with their start and end apart: 34, of which 32 were waited for; matrix products, arithmetic and copies ran while one was open for 23% of the time, Pallas kernels for 0%

commit v1 on v0

v1 whole, which is shorter than its diff:
```python
import functools
import math

import jax
import jax.numpy as jnp
from jax import lax
from jax.experimental import pallas as pl
from jax.experimental.pallas import tpu as pltpu
from jax.sharding import PartitionSpec as P

F32 = jnp.float32
BF16 = jnp.bfloat16
LANES = 128
SEGS = 8


def rows_at(i, steps):
    return pl.ds(i, SEGS, stride=steps)


def spread(row):
    return jnp.broadcast_to(row, (SEGS, LANES))


def segment_states(u_scr, decay_ref, pre_ref, end_ref, reverse):
    modes = decay_ref.shape[0]
    steps = u_scr.shape[0] // SEGS
    a = [spread(jnp.exp(-decay_ref[r : r + 1, :])) for r in range(modes)]

    def step(k, states):
        i = steps - 1 - k if reverse else k
        u = u_scr[rows_at(i, steps), :]
        return tuple(a[r] * states[r] + u for r in range(modes))

    zero = jnp.zeros((SEGS, LANES), F32)
    states = lax.fori_loop(0, steps, step, (zero,) * modes, unroll=4)
    seg = lax.broadcasted_iota(jnp.int32, (SEGS, LANES), 0)

    def moved(x, by):
        if reverse:
            return jnp.where(seg < SEGS - by, pltpu.roll(x, SEGS - by, 0), 0.0)
        return jnp.where(seg >= by, pltpu.roll(x, by, 0), 0.0)

    last = 0 if reverse else SEGS - 1
    for r in range(modes):
        rate = spread(decay_ref[r : r + 1, :])
        x = states[r]
        for by in (1, 2, 4):
            x = x + jnp.exp(-rate * float(steps * by)) * moved(x, by)
        end_ref[r : r + 1, :] = x[last : last + 1, :]
        pre_ref[r] = moved(x, 1)


def full_scan(u_scr, y_scr, decay_ref, res_ref, pre_ref, ends_ref, reverse):
    modes = decay_ref.shape[0]
    rows = u_scr.shape[0]
    steps = rows // SEGS
    ctx = ends_ref.shape[0]
    me = lax.axis_index("ctx")
    whole = jnp.exp(-decay_ref[...] * float(rows))

    def add_device(k, incoming):
        j = ctx - 1 - k if reverse else k
        before = j > me if reverse else j < me
        return jnp.where(before, whole * incoming + ends_ref[j], incoming)

    incoming = lax.fori_loop(0, ctx, add_device, jnp.zeros(decay_ref.shape, F32))
    seg = lax.broadcasted_iota(jnp.int32, (SEGS, LANES), 0)
    ahead = ((SEGS - 1 - seg if reverse else seg) * steps).astype(F32)
    a = []
    first = []
    for r in range(modes):
        rate = spread(decay_ref[r : r + 1, :])
        a.append(jnp.exp(-rate))
        first.append(pre_ref[r] + jnp.exp(-rate * ahead) * incoming[r : r + 1, :])
    res = [spread(res_ref[r : r + 1, :]) for r in range(modes)]

    def step(k, states):
        i = steps - 1 - k if reverse else k
        u = u_scr[rows_at(i, steps), :]
        states = tuple(a[r] * states[r] + u for r in range(modes))
        terms = [res[r] * states[r] for r in range(modes)]
        while len(terms) > 1:
            terms = [p + q for p, q in zip(terms[::2], terms[1::2])]
        y_scr[rows_at(i, steps), :] = terms[0]
        return states

    lax.fori_loop(0, steps, step, tuple(first), unroll=2)


def forward_ends(inner_ref, values_ref, decay_ref, pre_ref, end_ref, u_scr):
    u_scr[...] = inner_ref[...].astype(F32) * values_ref[...].astype(F32)
    segment_states(u_scr, decay_ref, pre_ref, end_ref, False)


def forward_finish(
    inner_ref, values_ref, outer_ref, decay_ref, res_ref, skip_ref, pre_ref, ends_ref,
    filtered_ref, modulated_ref, u_scr, y_scr,
):
    u_scr[...] = inner_ref[...].astype(F32) * values_ref[...].astype(F32)
    full_scan(u_scr, y_scr, decay_ref, res_ref, pre_ref, ends_ref, False)
    filtered = y_scr[...] + skip_ref[...] * u_scr[...]
    filtered_ref[...] = filtered
    modulated_ref[...] = (outer_ref[...].astype(F32) * filtered).astype(BF16)


def backward_ends(grad_ref, outer_ref, decay_ref, pre_ref, end_ref, u_scr):
    u_scr[...] = grad_ref[...].astype(F32) * outer_ref[...].astype(F32)
    segment_states(u_scr, decay_ref, pre_ref, end_ref, True)


def backward_finish(
    grad_ref, outer_ref, inner_ref, values_ref, filtered_ref, decay_ref, res_ref, skip_ref,
    pre_ref, ends_ref, outer_grad_ref, inner_grad_ref, value_grad_ref, u_scr, y_scr,
):
    grad = grad_ref[...].astype(F32)
    u_scr[...] = grad * outer_ref[...].astype(F32)
    outer_grad_ref[...] = (grad * filtered_ref[...]).astype(BF16)
    full_scan(u_scr, y_scr, decay_ref, res_ref, pre_ref, ends_ref, True)
    gated_grad = y_scr[...] + skip_ref[...] * u_scr[...]
    inner_grad_ref[...] = (gated_grad * values_ref[...].astype(F32)).astype(BF16)
    value_grad_ref[...] = (gated_grad * inner_ref[...].astype(F32)).astype(BF16)


def by_lanes(kernel, operands, outs, rows, scans):
    channels = operands[0].shape[-1]

    def spec(x):
        lead = x.shape[:-1]
        return pl.BlockSpec(lead + (LANES,), lambda c, n=len(lead): (0,) * n + (c,))

    work = rows * channels * 16 * (6 if scans > 1 else 2)
    moved = sum(math.prod(x.shape) * x.dtype.itemsize for x in list(operands) + list(outs))
    return pl.pallas_call(
        kernel,
        grid=(channels // LANES,),
        out_shape=outs,
        in_specs=[spec(x) for x in operands],
        out_specs=[spec(x) for x in outs],
        scratch_shapes=[pltpu.VMEM((rows, LANES), F32)] * scans,
        cost_estimate=pl.CostEstimate(flops=work, bytes_accessed=moved, transcendentals=0),
        name=kernel.__name__,
    )(*operands)


def shards(outer_gate, inner_gate, values, out_weight, skip_gain, residues, decay_rates, out_grad):
    rows, channels = values.shape
    modes = decay_rates.shape[1]
    ctx = lax.axis_size("ctx")
    shape = jax.ShapeDtypeStruct
    panel = lax.all_gather(out_weight, "ctx", axis=0, tiled=True)
    decay = decay_rates.T
    res = residues.T
    skip = skip_gain[None]
    state_outs = [shape((modes, SEGS, channels), F32), shape((modes, channels), F32)]
    pre, end = by_lanes(forward_ends, (inner_gate, values, decay), state_outs, rows, 1)
    ends = lax.all_gather(end, "ctx", axis=0)
    filtered, modulated = by_lanes(
        forward_finish,
        (inner_gate, values, outer_gate, decay, res, skip, pre, ends),
        [shape((rows, channels), F32), shape((rows, channels), BF16)],
        rows,
        2,
    )
    gathered = lax.all_gather(modulated, "fsdp", axis=1, tiled=True)
    grad_rows = lax.dot_general(
        gathered, out_grad, (((0,), (0,)), ((), ())), preferred_element_type=F32
    ).astype(BF16)
    weight_grad = lax.psum_scatter(grad_rows, "ctx", scatter_dimension=0, tiled=True)
    weight_grad = weight_grad.astype(F32) * (1.0 / math.sqrt(rows * ctx))
    block_out = jnp.dot(gathered, panel, preferred_element_type=F32).astype(BF16)
    partial = jnp.dot(out_grad, panel.T, preferred_element_type=F32).astype(BF16)
    grad = lax.psum_scatter(partial, "fsdp", scatter_dimension=1, tiled=True)
    pre, end = by_lanes(backward_ends, (grad, outer_gate, decay), state_outs, rows, 1)
    ends = lax.all_gather(end, "ctx", axis=0)
    outer_grad, inner_grad, value_grad = by_lanes(
        backward_finish,
        (grad, outer_gate, inner_gate, values, filtered, decay, res, skip, pre, ends),
        [shape((rows, channels), BF16)] * 3,
        rows,
        2,
    )
    return (block_out, outer_grad, inner_grad, value_grad, weight_grad)


def solution(mesh):
    tile = P("ctx", "fsdp")
    return jax.shard_map(
        shards,
        mesh=mesh,
        in_specs=(tile, tile, tile, tile, P("fsdp"), P("fsdp", None), P("fsdp", None), tile),
        out_specs=(tile,) * 5,
        check_vma=False,
    )
```

time: 633 us -> 312 us (0.49); the launches traced: 624 us -> 311 us
  matrix products: 168 us -> 17.5 us
  local copies, waits for them, and re-layouts: 96.3 us -> 0.01 us
  starting transfers between devices: 93.9 us -> 0.24 us
  Pallas kernels: 0 us -> 40.4 us
  other arithmetic: 17.8 us -> 1.8 us
    dot_general x9 -> x3, matrix products: 168 us -> 17.5 us  [the longest x1 5.96 us: shards(): lax.dot_general(gathered, out_grad, (((0,), (0,)), ((), ())), preferred_e...]
    all_gather x2 -> x4, waiting for transfers between devices: 41.8 us -> 145 us  [the longest x2 77.8 us: shards(): ends = lax.all_gather(end, 'ctx', axis=0)]
    ppermute x30 -> x0, starting transfers between devices: 93.7 us -> none  [passed_along(): return lax.ppermute(block, axis, route)]
    ppermute x30 -> x0, waiting for transfers between devices: 91.9 us -> none  [passed_along(): return lax.ppermute(block, axis, route)]
    gather x2 -> x0, local copies, waits for them, and re-layouts: 49.1 us -> none  [mode_tables(): picked = kernel[:, jnp.clip(lag_index, 0, block_rows - 1)]]
    pallas_call x0 -> x4, Pallas kernels: none -> 40.4 us  [by_lanes(): pl.pallas_call(kernel, grid=(channels // LANES,), out_shape=outs, in_spec...]
    reduce_scatter x1, waiting for transfers between devices: 97.8 us -> 63 us  [shards(): lax.psum_scatter(grad_rows, 'ctx', scatter_dimension=0, tiled=True)]
    reduce_scatter x1, waiting for transfers between devices: 0.01 us -> 27.9 us  [shards(): grad = lax.psum_scatter(partial, 'fsdp', scatter_dimension=1, tiled=True)]
  transfers between devices with their start and end apart: 34 -> 6, of which waited for: 32 -> 6; matrix products, arithmetic and copies ran while one was open for 23% -> 6% of each run, Pallas kernels for 0% -> 6%
where the time goes in v1:
time: 312 us; the launch traced here: 311 us
  waiting for transfers between devices  237 us (76%)
  Pallas kernels  40.4 us (13%)
  matrix products  17.5 us (6%)
  between operations  14.1 us (5%)
    all_gather x2, waiting for transfers between devices, shards(): ends = lax.all_gather(end, 'ctx', axis=0)  77.8 us
    reduce_scatter x1, waiting for transfers between devices, shards(): lax.psum_scatter(grad_rows, 'ctx', scatter_dimension=0, tiled=True)  63 us
    pallas_call x4, Pallas kernels, by_lanes(): pl.pallas_call(kernel, grid=(channels // LANES,), out_shape=outs, in_spec...  40.4 us
    all_gather x1, waiting for transfers between devices, shards(): panel = lax.all_gather(out_weight, 'ctx', axis=0, tiled=True)  39.5 us
    reduce_scatter x1, waiting for transfers between devices, shards(): grad = lax.psum_scatter(partial, 'fsdp', scatter_dimension=1, tiled=True)  27.9 us
    all_gather x1, waiting for transfers between devices, shards(): gathered = lax.all_gather(modulated, 'fsdp', axis=1, tiled=True)  27.8 us
  transfers between devices with their start and end apart: 6, of which 6 were waited for; matrix products, arithmetic and copies ran while one was open for 6% of the time, Pallas kernels for 6%

profile of v1, /device:TPU:0, one launch (start us, length us, event | category | flops | bytes accessed | tf_op | source)
XLA Modules:
  0.0 310.9 jit_solution(2779077024213161869)
XLA Ops:
  7.2 0.0 copy-start
  7.2 0.0 all-gather.11.cloned.1.call-start
  7.2 7.9 %forward_ends.1 = (f32[16,8,1024]{2,1,0:T(8,128)}, f32[16,1024]{1,0:T(8,128)}) custom-call(bf16[512,1024]{1,0:T(8,128)(2,1)} %inner_ref.5, bf16[512,1024]{1,0:T(8,128)(2,1)} %values_ref.5, f32[16,1024]{1,0:T(8,128)} %bitcast.11), custom_call_target="tpu_custom_call" | custom-call | flops 16777216 | bytes 2752512 | tf_op jit(solution)/shard_map/forward_ends/pallas_call | solution.py:134
  15.1 0.0 all-gather.11.cloned.1.call-update
  15.1 0.0 all-gather.9.cloned.1.call-start
  15.2 0.7 all-gather.9.cloned.1.call-update
  15.9 0.0 all-gather.7.cloned.1.call-start
  15.9 40.0 %all-gather.11.cloned.1.call-done = f32[256,1024]{1,0:T(8,128)} async-done(((f32[16,1024]{1,0:T(8,128)}), f32[256,1024]{1,0:T(8,128)}) %all-gather.11.cloned.1.call-update) | async-done | bytes 1048592 | tf_op jit(solution)/shard_map/all_gather | solution.py:157
  55.9 12.2 %forward_finish.1 = (f32[512,1024]{1,0:T(8,128)}, bf16[512,1024]{1,0:T(8,128)(2,1)}) custom-call(bf16[512,1024]{1,0:T(8,128)(2,1)} %inner_ref.5, bf16[512,1024]{1,0:T(8,128)(2,1)} %values_ref.5, bf16[512,1024]{1,0:T(8,128)(2,1)} %outer_ref.5, f32[16,1024]{1,0:T(8,128)} %bitcast.12, f32[16,1024]{1,0:T(8,128)} %bitcast.17, f32[1,1024]{1,0:T(1,128)} %bitcast.19, ...), custom_call_target="tpu_custom_call" | custom-call | flops 50331648 | bytes 7999488 | tf_op jit(solution)/shard_map/forward_finish/pallas_call | solution.py:134
  68.2 0.0 all-gather.7.cloned.1.call-update
  68.2 0.0 reduce-scatter.3.cloned.1.call-start
  68.2 39.5 %all-gather.9.cloned.1.call-done = bf16[2048,1024]{1,0:T(8,128)(2,1)} async-done(((bf16[128,1024]{1,0:T(8,128)(2,1)}), bf16[2048,1024]{1,0:T(8,128)(2,1)}) %all-gather.9.cloned.1.call-update) | async-done | bytes 4194320 | tf_op jit(solution)/shard_map/all_gather | solution.py:151
  107.7 0.0 copy-done
  107.7 5.9 %convolution_convert_fusion.1 = bf16[512,2048]{1,0:T(8,128)(2,1)} fusion(bf16[512,1024]{1,0:T(8,128)(2,1)S(1)} %copy-done, bf16[2048,1024]{1,0:T(8,128)(2,1)} %all-gather.9.cloned.1.call-done), kind=kOutput, calls=%fused_computation.1 | convolution fusion | flops 2148532224 | bytes 7340032 | tf_op jit(solution)/shard_map/dot_general | solution.py:172
  113.6 0.0 reduce-scatter.3.cloned.1.call-update
  113.7 0.0 reduce-scatter.5.cloned.1.call-start
  113.7 27.8 %all-gather.7.cloned.1.call-done = bf16[512,2048]{1,0:T(8,128)(2,1)} async-done(((bf16[512,1024]{1,0:T(8,128)(2,1)}), bf16[512,2048]{1,0:T(8,128)(2,1)}) %all-gather.7.cloned.1.call-update) | async-done | bytes 2097168 | tf_op jit(solution)/shard_map/all_gather | solution.py:165
  141.5 6.0 %convolution_convert_fusion = bf16[2048,1024]{1,0:T(8,128)(2,1)} fusion(bf16[512,2048]{1,0:T(8,128)(2,1)} %all-gather.7.cloned.1.call-done, bf16[512,1024]{1,0:T(8,128)(2,1)S(1)} %copy-done), kind=kOutput, calls=%fused_computation | convolution fusion | flops 2149580800 | bytes 7340032 | tf_op jit(solution)/shard_map/dot_general | solution.py:166
  147.5 0.0 copy-start.1
  147.5 0.0 reduce-scatter.5.cloned.1.call-update
  147.5 0.0 all-gather.13.cloned.1.call-start
  147.5 27.9 %reduce-scatter.3.cloned.1.call-done.grad_ref = bf16[512,1024]{1,0:T(8,128)(2,1)} async-done(((bf16[512,2048]{1,0:T(8,128)(2,1)}), bf16[512,1024]{1,0:T(8,128)(2,1)}) %reduce-scatter.3.cloned.1.call-update) | async-done | bytes 1048592 | tf_op jit(solution)/shard_map/reduce_scatter | solution.py:173
  175.5 7.9 %backward_ends.1 = (f32[16,8,1024]{2,1,0:T(8,128)}, f32[16,1024]{1,0:T(8,128)}) custom-call(bf16[512,1024]{1,0:T(8,128)(2,1)} %reduce-scatter.3.cloned.1.call-done.grad_ref, bf16[512,1024]{1,0:T(8,128)(2,1)} %outer_ref.5, f32[16,1024]{1,0:T(8,128)} %bitcast.13), custom_call_target="tpu_custom_call" | custom-call | flops 16777216 | bytes 2752512 | tf_op jit(solution)/shard_map/backward_ends/pallas_call | solution.py:134
  183.4 0.0 all-gather.13.cloned.1.call-update
  183.4 0.0 copy-done.1
  183.4 5.7 %convolution_convert_fusion.2 = bf16[512,1024]{1,0:T(8,128)(2,1)} fusion(bf16[512,2048]{1,0:T(8,128)(2,1)S(1)} %copy-done.1, bf16[2048,1024]{1,0:T(8,128)(2,1)} %all-gather.9.cloned.1.call-done), kind=kOutput, calls=%fused_computation.2 | convolution fusion | flops 2148007936 | bytes 7340032 | tf_op jit(solution)/shard_map/dot_general | solution.py:171
  189.1 63.0 %reduce-scatter.5.cloned.1.call-done = bf16[128,1024]{1,0:T(8,128)(2,1)} async-done(((bf16[2048,1024]{1,0:T(8,128)(2,1)}), bf16[128,1024]{1,0:T(8,128)(2,1)}) %reduce-scatter.5.cloned.1.call-update) | async-done | bytes 262160 | tf_op jit(solution)/shard_map/reduce_scatter | solution.py:169
  252.1 1.8 convert_multiply_fusion
  253.9 37.8 %all-gather.13.cloned.1.call-done = f32[256,1024]{1,0:T(8,128)} async-done(((f32[16,1024]{1,0:T(8,128)}), f32[256,1024]{1,0:T(8,128)}) %all-gather.13.cloned.1.call-update) | async-done | bytes 1048592 | tf_op jit(solution)/shard_map/all_gather | solution.py:175
  291.7 12.4 %backward_finish.1 = (bf16[512,1024]{1,0:T(8,128)(2,1)}, bf16[512,1024]{1,0:T(8,128)(2,1)}, bf16[512,1024]{1,0:T(8,128)(2,1)}) custom-call(bf16[512,1024]{1,0:T(8,128)(2,1)} %reduce-scatter.3.cloned.1.call-done.grad_ref, bf16[512,1024]{1,0:T(8,128)(2,1)} %outer_ref.5, bf16[512,1024]{1,0:T(8,128)(2,1)} %inner_ref.5, bf16[512,1024]{1,0:T(8,128)(2,1)} %values_ref.5, ...), custom_call_target="tpu_custom_call" | custom-call | flops 50331648 | bytes 11145216 | tf_op jit(solution)/shard_map/backward_finish/pallas_call | solution.py:134
Async XLA Ops:
  7.2 100.6 %copy-start = (bf16[512,1024]{1,0:T(8,128)(2,1)S(1)}, bf16[512,1024]{1,0:T(8,128)(2,1)}, u32[]{:S(2)}) copy-start(bf16[512,1024]{1,0:T(8,128)(2,1)} %param.15) | copy-start | bytes 3145732
  7.2 48.7 %all-gather.11.cloned.1.call-start = ((), (), s32[]{:S(2)}) async-start(), calls=%async_computation.6 | async-start | bytes 1114112 | tf_op jit(solution)/shard_map/all_gather | solution.py:157
  15.1 92.6 %all-gather.9.cloned.1.call-start = ((), (), s32[]{:S(2)}) async-start(), calls=%async_computation.3 | async-start | bytes 4456448 | tf_op jit(solution)/shard_map/all_gather | solution.py:151
  15.9 125.6 %all-gather.7.cloned.1.call-start = ((), (), s32[]{:S(2)}) async-start(), calls=%async_computation.2 | async-start | bytes 3145728 | tf_op jit(solution)/shard_map/all_gather | solution.py:165
  68.2 107.3 %reduce-scatter.3.cloned.1.call-start = ((), (), s32[]{:S(2)}) async-start(), calls=%async_computation.4 | async-start | bytes 3145728 | tf_op jit(solution)/shard_map/reduce_scatter | solution.py:173
  113.7 138.4 %reduce-scatter.5.cloned.1.call-start = ((), (), s32[]{:S(2)}) async-start(), calls=%async_computation.5 | async-start | bytes 4456448 | tf_op jit(solution)/shard_map/reduce_scatter | solution.py:169
  147.5 35.9 %copy-start.1 = (bf16[512,2048]{1,0:T(8,128)(2,1)S(1)}, bf16[512,2048]{1,0:T(8,128)(2,1)}, u32[]{:S(2)}) copy-start(bf16[512,2048]{1,0:T(8,128)(2,1)} %all-gather.7.cloned.1.call-done) | copy-start | bytes 6291460
  147.5 144.2 %all-gather.13.cloned.1.call-start = ((), (), s32[]{:S(2)}) async-start(), calls=%async_computation.7 | async-start | bytes 1114112 | tf_op jit(solution)/shard_map/all_gather | solution.py:175
Sparse Core Ops, SparseCore 0:
  15.2 40.6 all-gather.10
  58.1 49.6 all-gather.8
  109.9 31.5 all-gather.6
  143.6 31.8 reduce-scatter.2
  179.7 72.3 reduce-scatter.4
  254.6 37.0 all-gather.12

commit v2 on v1

--- a/solution.py
+++ b/solution.py
@@ -51,20 +51,10 @@
         pre_ref[r] = moved(x, 1)
 
 
-def full_scan(u_scr, y_scr, decay_ref, res_ref, pre_ref, ends_ref, reverse):
+def full_scan(u_scr, y_scr, decay_ref, res_ref, pre_ref, incoming_ref, reverse):
     modes = decay_ref.shape[0]
     rows = u_scr.shape[0]
     steps = rows // SEGS
-    ctx = ends_ref.shape[0]
-    me = lax.axis_index("ctx")
-    whole = jnp.exp(-decay_ref[...] * float(rows))
-
-    def add_device(k, incoming):
-        j = ctx - 1 - k if reverse else k
-        before = j > me if reverse else j < me
-        return jnp.where(before, whole * incoming + ends_ref[j], incoming)
-
-    incoming = lax.fori_loop(0, ctx, add_device, jnp.zeros(decay_ref.shape, F32))
     seg = lax.broadcasted_iota(jnp.int32, (SEGS, LANES), 0)
     ahead = ((SEGS - 1 - seg if reverse else seg) * steps).astype(F32)
     a = []
@@ -72,7 +62,7 @@
     for r in range(modes):
         rate = spread(decay_ref[r : r + 1, :])
         a.append(jnp.exp(-rate))
-        first.append(pre_ref[r] + jnp.exp(-rate * ahead) * incoming[r : r + 1, :])
+        first.append(pre_ref[r] + jnp.exp(-rate * ahead) * incoming_ref[r : r + 1, :])
     res = [spread(res_ref[r : r + 1, :]) for r in range(modes)]
 
     def step(k, states):
@@ -94,29 +84,30 @@
 
 
 def forward_finish(
-    inner_ref, values_ref, outer_ref, decay_ref, res_ref, skip_ref, pre_ref, ends_ref,
+    inner_ref, values_ref, outer_ref, decay_ref, res_ref, skip_ref, pre_ref, incoming_ref,
     filtered_ref, modulated_ref, u_scr, y_scr,
 ):
     u_scr[...] = inner_ref[...].astype(F32) * values_ref[...].astype(F32)
-    full_scan(u_scr, y_scr, decay_ref, res_ref, pre_ref, ends_ref, False)
+    full_scan(u_scr, y_scr, decay_ref, res_ref, pre_ref, incoming_ref, False)
     filtered = y_scr[...] + skip_ref[...] * u_scr[...]
     filtered_ref[...] = filtered
     modulated_ref[...] = (outer_ref[...].astype(F32) * filtered).astype(BF16)
 
 
-def backward_ends(grad_ref, outer_ref, decay_ref, pre_ref, end_ref, u_scr):
-    u_scr[...] = grad_ref[...].astype(F32) * outer_ref[...].astype(F32)
+def backward_ends(own_ref, other_ref, outer_ref, decay_ref, pre_ref, end_ref, u_scr):
+    grad = own_ref[...].astype(F32) + other_ref[...].astype(F32)
+    u_scr[...] = grad * outer_ref[...].astype(F32)
     segment_states(u_scr, decay_ref, pre_ref, end_ref, True)
 
 
 def backward_finish(
-    grad_ref, outer_ref, inner_ref, values_ref, filtered_ref, decay_ref, res_ref, skip_ref,
-    pre_ref, ends_ref, outer_grad_ref, inner_grad_ref, value_grad_ref, u_scr, y_scr,
+    own_ref, other_ref, outer_ref, inner_ref, values_ref, filtered_ref, decay_ref, res_ref, skip_ref,
+    pre_ref, incoming_ref, outer_grad_ref, inner_grad_ref, value_grad_ref, u_scr, y_scr,
 ):
-    grad = grad_ref[...].astype(F32)
+    grad = own_ref[...].astype(F32) + other_ref[...].astype(F32)
     u_scr[...] = grad * outer_ref[...].astype(F32)
     outer_grad_ref[...] = (grad * filtered_ref[...]).astype(BF16)
-    full_scan(u_scr, y_scr, decay_ref, res_ref, pre_ref, ends_ref, True)
+    full_scan(u_scr, y_scr, decay_ref, res_ref, pre_ref, incoming_ref, True)
     gated_grad = y_scr[...] + skip_ref[...] * u_scr[...]
     inner_grad_ref[...] = (gated_grad * values_ref[...].astype(F32)).astype(BF16)
     value_grad_ref[...] = (gated_grad * inner_ref[...].astype(F32)).astype(BF16)
@@ -143,10 +134,67 @@
     )(*operands)
 
 
+def prefix_kernel(reverse, rows, end_ref, decay_ref, out_ref, sent, got, send_sem, recv_sem):
+    me, n = lax.axis_index("ctx"), lax.axis_size("ctx")
+    hops = [1 << k for k in range(sent.shape[0])]
+    barrier = pltpu.get_barrier_semaphore()
+    for hop in hops:
+        for peer in (lax.rem(me + hop, n), lax.rem(me + n - hop, n)):
+            pl.semaphore_signal(
+                barrier, inc=1, device_id={"ctx": peer}, device_id_type=pl.DeviceIdType.MESH
+            )
+    pl.semaphore_wait(barrier, 2 * len(hops))
+    decay = decay_ref[...]
+    upto = end_ref[...]
+    before = jnp.zeros_like(upto)
+    for k, hop in enumerate(hops):
+        sent[k] = upto
+        copy = pltpu.make_async_remote_copy(
+            src_ref=sent.at[k],
+            dst_ref=got.at[k],
+            send_sem=send_sem.at[k],
+            recv_sem=recv_sem.at[k],
+            device_id={"ctx": lax.rem(me + (n - hop if reverse else hop), n)},
+            device_id_type=pl.DeviceIdType.MESH,
+        )
+        copy.start()
+        near = jnp.exp(-decay * float(rows * (hop - 1)))
+        far = jnp.exp(-decay * float(rows * hop))
+        copy.wait()
+        inside = (me + hop < n) if reverse else (me >= hop)
+        term = got[k] * jnp.where(inside, 1.0, 0.0)
+        before = before + near * term
+        upto = upto + far * term
+    out_ref[...] = before
+
+
+def prefix(end, decay, rows, reverse):
+    hops = max(1, (lax.axis_size("ctx") - 1).bit_length())
+    whole = pl.BlockSpec(memory_space=pltpu.VMEM)
+    return pl.pallas_call(
+        functools.partial(prefix_kernel, reverse, rows),
+        out_shape=jax.ShapeDtypeStruct(end.shape, F32),
+        in_specs=[whole, whole],
+        out_specs=whole,
+        scratch_shapes=[
+            pltpu.VMEM((hops,) + end.shape, F32),
+            pltpu.VMEM((hops,) + end.shape, F32),
+            pltpu.SemaphoreType.DMA((hops,)),
+            pltpu.SemaphoreType.DMA((hops,)),
+        ],
+        compiler_params=pltpu.CompilerParams(
+            collective_id=2 if reverse else 1, has_side_effects=True
+        ),
+        name="prefix_back" if reverse else "prefix_ahead",
+    )(end, decay)
+
+
 def shards(outer_gate, inner_gate, values, out_weight, skip_gain, residues, decay_rates, out_grad):
     rows, channels = values.shape
     modes = decay_rates.shape[1]
-    ctx = lax.axis_size("ctx")
+    ctx, fsdp = lax.axis_size("ctx"), lax.axis_size("fsdp")
+    at = lax.axis_index("fsdp")
+    swap = [(0, 1), (1, 0)]
     shape = jax.ShapeDtypeStruct
     panel = lax.all_gather(out_weight, "ctx", axis=0, tiled=True)
     decay = decay_rates.T
@@ -154,28 +202,42 @@
     skip = skip_gain[None]
     state_outs = [shape((modes, SEGS, channels), F32), shape((modes, channels), F32)]
     pre, end = by_lanes(forward_ends, (inner_gate, values, decay), state_outs, rows, 1)
-    ends = lax.all_gather(end, "ctx", axis=0)
+    incoming = prefix(end, decay, rows, False)
     filtered, modulated = by_lanes(
         forward_finish,
-        (inner_gate, values, outer_gate, decay, res, skip, pre, ends),
+        (inner_gate, values, outer_gate, decay, res, skip, pre, incoming),
         [shape((rows, channels), F32), shape((rows, channels), BF16)],
         rows,
         2,
     )
-    gathered = lax.all_gather(modulated, "fsdp", axis=1, tiled=True)
+    if fsdp == 2:
+        other = lax.ppermute(modulated, "fsdp", swap)
+        first = jnp.where(at == 0, modulated, other)
+        second = jnp.where(at == 0, other, modulated)
+        gathered = jnp.concatenate([first, second], axis=1)
+        mine = lax.dynamic_slice_in_dim(panel, at * channels, channels, 0)
+        theirs = lax.dynamic_slice_in_dim(panel, (1 - at) * channels, channels, 0)
+        for_them = jnp.dot(out_grad, theirs.T, preferred_element_type=F32).astype(BF16)
+        from_them = lax.ppermute(for_them, "fsdp", swap)
+        own = jnp.dot(out_grad, mine.T, preferred_element_type=F32).astype(BF16)
+    else:
+        gathered = lax.all_gather(modulated, "fsdp", axis=1, tiled=True)
+        partial = jnp.dot(out_grad, panel.T, preferred_element_type=F32).astype(BF16)
+        own = lax.psum_scatter(partial, "fsdp", scatter_dimension=1, tiled=True)
+        from_them = jnp.zeros_like(own)
     grad_rows = lax.dot_general(
         gathered, out_grad, (((0,), (0,)), ((), ())), preferred_element_type=F32
     ).astype(BF16)
     weight_grad = lax.psum_scatter(grad_rows, "ctx", scatter_dimension=0, tiled=True)
     weight_grad = weight_grad.astype(F32) * (1.0 / math.sqrt(rows * ctx))
     block_out = jnp.dot(gathered, panel, preferred_element_type=F32).astype(BF16)
-    partial = jnp.dot(out_grad, panel.T, preferred_element_type=F32).astype(BF16)
-    grad = lax.psum_scatter(partial, "fsdp", scatter_dimension=1, tiled=True)
-    pre, end = by_lanes(backward_ends, (grad, outer_gate, decay), state_outs, rows, 1)
-    ends = lax.all_gather(end, "ctx", axis=0)
+    pre, end = by_lanes(
+        backward_ends, (own, from_them, outer_gate, decay), state_outs, rows, 1
+    )
+    incoming = prefix(end, decay, rows, True)
     outer_grad, inner_grad, value_grad = by_lanes(
         backward_finish,
-        (grad, outer_gate, inner_gate, values, filtered, decay, res, skip, pre, ends),
+        (own, from_them, outer_gate, inner_gate, values, filtered, decay, res, skip, pre, incoming),
         [shape((rows, channels), BF16)] * 3,
         rows,
         2,

time: 312 us -> 209 us (0.67)
  waiting for transfers between devices: 237 us -> 88.3 us
  Pallas kernels: 40.4 us -> 83.3 us
    all_gather x3 -> x0, waiting for transfers between devices: 106 us -> none  [the longest x2 77.8 us: shards(): ends = lax.all_gather(end, 'ctx', axis=0)]
    pallas_call x0 -> x2, Pallas kernels: none -> 43.8 us  [prefix(): pl.pallas_call(functools.partial(prefix_kernel, reverse, rows), out_shape...]
    all_gather x1, waiting for transfers between devices: 39.5 us -> 0.02 us  [shards(): panel = lax.all_gather(out_weight, 'ctx', axis=0, tiled=True)]
    reduce_scatter x1 -> x0, waiting for transfers between devices: 27.9 us -> none  [shards(): grad = lax.psum_scatter(partial, 'fsdp', scatter_dimension=1, tiled=True)]
    ppermute x0 -> x2, waiting for transfers between devices: none -> 21.4 us  [the longest x1 21.4 us: shards(): other = lax.ppermute(modulated, 'fsdp', swap)]
    reduce_scatter x1, waiting for transfers between devices: 63 us -> 66.1 us  [shards(): lax.psum_scatter(grad_rows, 'ctx', scatter_dimension=0, tiled=True)]
    dot_general x1 -> x2, matrix products: 5.9 us -> 7.85 us  [the longest x1 4 us: shards(): own = jnp.dot(out_grad, mine.T, preferred_element_type=F32).astype(BF16)]
  transfers between devices with their start and end apart: 6 -> 4, of which waited for: 6 -> 2; matrix products, arithmetic and copies ran while one was open for 6% -> 9% of each run, Pallas kernels for 6% -> 22%
where the time goes in v2:
time: 209 us; the launch traced here: 208 us
  waiting for transfers between devices  88.3 us (42%)
  Pallas kernels  83.3 us (40%)
  matrix products  15.5 us (7%)
  between operations  14.1 us (7%)
  other arithmetic  3.48 us (2%)
  starting transfers between devices  2.56 us (1%)
    reduce_scatter x1, waiting for transfers between devices, shards(): lax.psum_scatter(grad_rows, 'ctx', scatter_dimension=0, tiled=True)  66.1 us
    pallas_call x2, Pallas kernels, prefix(): pl.pallas_call(functools.partial(prefix_kernel, reverse, rows), out_shape...  43.8 us
    pallas_call x4, Pallas kernels, by_lanes(): pl.pallas_call(kernel, grid=(channels // LANES,), out_shape=outs, in_spec...  39.5 us
    ppermute x1, waiting for transfers between devices, shards(): other = lax.ppermute(modulated, 'fsdp', swap)  21.4 us
    dot_general x1, matrix products, shards(): lax.dot_general(gathered, out_grad, (((0,), (0,)), ((), ())), preferred_e...  4.35 us
  transfers between devices with their start and end apart: 4, of which 2 were waited for; matrix products, arithmetic and copies ran while one was open for 9% of the time, Pallas kernels for 22%

profile of v2, /device:TPU:0, one launch (start us, length us, event | category | flops | bytes accessed | tf_op | source)
XLA Modules:
  0.0 208.3 jit_solution(4065237332119937251)
XLA Ops:
  7.2 0.0 copy-start
  7.2 0.0 all-gather.2.cloned.1.call-start
  7.2 0.7 all-gather.2.cloned.1.call-update
  7.9 0.0 reduce-scatter.2.cloned.1.call-start
  8.0 7.8 %forward_ends.1 = (f32[16,8,1024]{2,1,0:T(8,128)}, f32[16,1024]{1,0:T(8,128)}) custom-call(bf16[512,1024]{1,0:T(8,128)(2,1)} %inner_ref.5, bf16[512,1024]{1,0:T(8,128)(2,1)} %values_ref.5, f32[16,1024]{1,0:T(8,128)} %bitcast.11), custom_call_target="tpu_custom_call" | custom-call | flops 16777216 | bytes 2752512 | tf_op jit(solution)/shard_map/forward_ends/pallas_call | solution.py:125
  15.8 25.8 %prefix_ahead.1.incoming_ref = f32[16,1024]{1,0:T(8,128)} custom-call(f32[16,1024]{1,0:T(8,128)} %get-tuple-element.15.end_ref, f32[16,1024]{1,0:T(8,128)} %bitcast.12), custom_call_target="tpu_custom_call" | custom-call | tf_op jit(solution)/shard_map/prefix_ahead/pallas_call | solution.py:174
  41.5 11.5 %forward_finish.1 = (f32[512,1024]{1,0:T(8,128)}, bf16[512,1024]{1,0:T(8,128)(2,1)}) custom-call(bf16[512,1024]{1,0:T(8,128)(2,1)} %inner_ref.5, bf16[512,1024]{1,0:T(8,128)(2,1)} %values_ref.5, bf16[512,1024]{1,0:T(8,128)(2,1)} %outer_ref.5, f32[16,1024]{1,0:T(8,128)} %bitcast.13, f32[16,1024]{1,0:T(8,128)} %bitcast.17, f32[1,1024]{1,0:T(1,128)} %bitcast.19, ...), custom_call_target="tpu_custom_call" | custom-call | flops 50331648 | bytes 7016448 | tf_op jit(solution)/shard_map/forward_finish/pallas_call | solution.py:125
  53.0 0.8 collective-permute-start
  53.8 21.4 %collective-permute-done = bf16[512,1024]{1,0:T(8,128)(2,1)} collective-permute-done((bf16[512,1024]{1,0:T(8,128)(2,1)}, bf16[512,1024]{1,0:T(8,128)(2,1)}, u32[]{:S(2)}, u32[]{:S(2)}) %collective-permute-start) | collective-permute-done | bytes 1048608 | tf_op jit(solution)/shard_map/ppermute | solution.py:214
  75.2 1.7 broadcast_select_fusion.1
  76.9 0.0 copy-start.2
  76.9 0.0 copy-done
  76.9 4.3 %convolution_convert_fusion = bf16[2048,1024]{1,0:T(8,128)(2,1)} fusion(bf16[512,1024]{1,0:T(8,128)(2,1)S(1)} %copy-done, bf16[512,1024]{1,0:T(8,128)(2,1)S(1)} %get-tuple-element.24, bf16[512,1024]{1,0:T(8,128)(2,1)S(1)} %get-tuple-element.23), kind=kOutput, calls=%fused_computation | convolution fusion | flops 2153775104 | bytes 7340032 | tf_op jit(solution)/shard_map/dot_general | solution.py:228
  81.3 0.0 copy-done.2
  81.3 0.0 reduce-scatter.2.cloned.1.call-update
  81.3 0.0 all-gather.2.cloned.1.call-done
  81.3 3.9 %fusion.10 = bf16[512,1024]{1,0:T(8,128)(2,1)} fusion(bf16[512,1024]{1,0:T(8,128)(2,1)S(1)} %copy-done, bf16[2048,1024]{1,0:T(8,128)(2,1)} %all-gather.2.cloned.1.call-done, s32[]{:T(128)S(6)} %select_n.22), kind=kOutput, calls=%fused_computation.9 | convolution fusion | flops 1074266112 | bytes 4194308 | tf_op jit(solution)/shard_map/dot_general | solution.py:220
  85.2 1.7 collective-permute-start.1
  86.9 66.1 %reduce-scatter.2.cloned.1.call-done = bf16[128,1024]{1,0:T(8,128)(2,1)} async-done(((bf16[2048,1024]{1,0:T(8,128)(2,1)}), bf16[128,1024]{1,0:T(8,128)(2,1)}) %reduce-scatter.2.cloned.1.call-update) | async-done | bytes 262160 | tf_op jit(solution)/shard_map/reduce_scatter | solution.py:231
  153.0 1.8 convert_multiply_fusion
  154.8 0.0 copy-start.3
  154.8 0.0 copy-start.4
  154.8 4.0 %fusion.13.own_ref = bf16[512,1024]{1,0:T(8,128)(2,1)} fusion(bf16[512,1024]{1,0:T(8,128)(2,1)S(1)} %copy-done, bf16[2048,1024]{1,0:T(8,128)(2,1)} %all-gather.2.cloned.1.call-done, s32[]{:T(128)S(6)} %select_n.21), kind=kOutput, calls=%fused_computation.10 | convolution fusion | flops 1074266112 | bytes 4194308 | tf_op jit(solution)/shard_map/dot_general | solution.py:222
  158.8 0.0 copy-done.3
  158.8 0.0 copy-done.4
  158.8 3.3 %convolution_convert_fusion.1 = bf16[512,1024]{1,0:T(8,128)(2,1)} fusion(bf16[2048,1024]{1,0:T(8,128)(2,1)S(1)} %copy-done.4, bf16[512,1024]{1,0:T(8,128)(2,1)S(1)} %copy-done.3, bf16[512,1024]{1,0:T(8,128)(2,1)S(1)} %get-tuple-element.23), kind=kOutput, calls=%fused_computation.8 | convolution fusion | flops 2152202240 | bytes 7340032 | tf_op jit(solution)/shard_map/dot_general | solution.py:233
  162.2 0.0 collective-permute-done.1.other_ref
  162.2 0.0 copy-start.1
  162.2 1.0 copy-done.1
  163.2 8.3 %backward_ends.1 = (f32[16,8,1024]{2,1,0:T(8,128)}, f32[16,1024]{1,0:T(8,128)}) custom-call(bf16[512,1024]{1,0:T(8,128)(2,1)} %fusion.13.own_ref, bf16[512,1024]{1,0:T(8,128)(2,1)} %copy-done.1, bf16[512,1024]{1,0:T(8,128)(2,1)} %outer_ref.5, f32[16,1024]{1,0:T(8,128)} %bitcast.14), custom_call_target="tpu_custom_call" | custom-call | flops 16777216 | bytes 3801088 | tf_op jit(solution)/shard_map/backward_ends/pallas_call | solution.py:125
  171.4 18.1 %prefix_back.1.incoming_ref = f32[16,1024]{1,0:T(8,128)} custom-call(f32[16,1024]{1,0:T(8,128)} %get-tuple-element.19.end_ref, f32[16,1024]{1,0:T(8,128)} %bitcast.15), custom_call_target="tpu_custom_call" | custom-call | tf_op jit(solution)/shard_map/prefix_back/pallas_call | solution.py:174
  189.5 11.9 %backward_finish.1 = (bf16[512,1024]{1,0:T(8,128)(2,1)}, bf16[512,1024]{1,0:T(8,128)(2,1)}, bf16[512,1024]{1,0:T(8,128)(2,1)}) custom-call(bf16[512,1024]{1,0:T(8,128)(2,1)} %fusion.13.own_ref, bf16[512,1024]{1,0:T(8,128)(2,1)} %copy-done.1, bf16[512,1024]{1,0:T(8,128)(2,1)} %outer_ref.5, bf16[512,1024]{1,0:T(8,128)(2,1)} %inner_ref.5, ...), custom_call_target="tpu_custom_call" | custom-call | flops 50331648 | bytes 11210752 | tf_op jit(solution)/shard_map/backward_finish/pallas_call | solution.py:125
Async XLA Ops:
  7.2 69.8 %copy-start = (bf16[512,1024]{1,0:T(8,128)(2,1)S(1)}, bf16[512,1024]{1,0:T(8,128)(2,1)}, u32[]{:S(2)}) copy-start(bf16[512,1024]{1,0:T(8,128)(2,1)} %param.15) | copy-start | bytes 3145732
  7.2 74.1 %all-gather.2.cloned.1.call-start = ((), (), s32[]{:S(2)}) async-start(), calls=%async_computation.1 | async-start | bytes 4456448 | tf_op jit(solution)/shard_map/all_gather | solution.py:199
  7.9 145.1 %reduce-scatter.2.cloned.1.call-start = ((), (), s32[]{:S(2)}) async-start(), calls=%async_computation.2 | async-start | bytes 4456448 | tf_op jit(solution)/shard_map/reduce_scatter | solution.py:231
  53.0 22.2 %collective-permute-start = (bf16[512,1024]{1,0:T(8,128)(2,1)}, bf16[512,1024]{1,0:T(8,128)(2,1)}, u32[]{:S(2)}, u32[]{:S(2)}) collective-permute-start(bf16[512,1024]{1,0:T(8,128)(2,1)} %get-tuple-element.16), channel_id=1, source_target_pairs={{0,1},{1,0},{2,3},{3,2},{4,5},{5,4},{6,7},{7,6},{8,9},{9,8},{10,11... | collective-permute-start | bytes 3145736 | tf_op jit(solution)/shard_map/ppermute | solution.py:214
  76.9 4.4 %copy-start.2 = (bf16[512,1024]{1,0:T(8,128)(2,1)}, bf16[512,1024]{1,0:T(8,128)(2,1)S(1)}, u32[]{:S(2)}) copy-start(bf16[512,1024]{1,0:T(8,128)(2,1)S(1)} %get-tuple-element.24) | copy-start | bytes 3145732
  85.2 77.0 %collective-permute-start.1 = (bf16[512,1024]{1,0:T(8,128)(2,1)}, bf16[512,1024]{1,0:T(8,128)(2,1)S(1)}, u32[]{:S(2)}, u32[]{:S(2)}) collective-permute-start(bf16[512,1024]{1,0:T(8,128)(2,1)} %fusion.10), channel_id=1, source_target_pairs={{0,1},{1,0},{2,3},{3,2},{4,5},{5,4},{6,7},{7,6},{8,9},{9,8},{10,11... | collective-permute-start | bytes 3145736 | tf_op jit(solution)/shard_map/ppermute | solution.py:221
  154.8 4.0 %copy-start.3 = (bf16[512,1024]{1,0:T(8,128)(2,1)S(1)}, bf16[512,1024]{1,0:T(8,128)(2,1)}, u32[]{:S(2)}) copy-start(bf16[512,1024]{1,0:T(8,128)(2,1)} %copy-done.2) | copy-start | bytes 3145732
  154.8 4.0 %copy-start.4 = (bf16[2048,1024]{1,0:T(8,128)(2,1)S(1)}, bf16[2048,1024]{1,0:T(8,128)(2,1)}, u32[]{:S(2)}) copy-start(bf16[2048,1024]{1,0:T(8,128)(2,1)} %all-gather.2.cloned.1.call-done) | copy-start | bytes 12582916
  162.2 1.0 copy-start.1
Sparse Core Ops, SparseCore 0:
  10.2 55.9 all-gather.1
  81.4 71.5 reduce-scatter.1

commit v3 on v2

--- a/solution.py
+++ b/solution.py
@@ -120,7 +120,7 @@
         lead = x.shape[:-1]
         return pl.BlockSpec(lead + (LANES,), lambda c, n=len(lead): (0,) * n + (c,))
 
-    work = rows * channels * 16 * (6 if scans > 1 else 2)
+    work = rows * channels * (24000 if scans > 1 else 16000)
     moved = sum(math.prod(x.shape) * x.dtype.itemsize for x in list(operands) + list(outs))
     return pl.pallas_call(
         kernel,
@@ -185,6 +185,7 @@
         compiler_params=pltpu.CompilerParams(
             collective_id=2 if reverse else 1, has_side_effects=True
         ),
+        cost_estimate=pl.CostEstimate(flops=18 * 10**9, bytes_accessed=0, transcendentals=0),
         name="prefix_back" if reverse else "prefix_ahead",
     )(end, decay)
 
@@ -229,7 +230,6 @@
         gathered, out_grad, (((0,), (0,)), ((), ())), preferred_element_type=F32
     ).astype(BF16)
     weight_grad = lax.psum_scatter(grad_rows, "ctx", scatter_dimension=0, tiled=True)
-    weight_grad = weight_grad.astype(F32) * (1.0 / math.sqrt(rows * ctx))
     block_out = jnp.dot(gathered, panel, preferred_element_type=F32).astype(BF16)
     pre, end = by_lanes(
         backward_ends, (own, from_them, outer_gate, decay), state_outs, rows, 1
@@ -242,6 +242,8 @@
         rows,
         2,
     )
+    weight_grad, value_grad = lax.optimization_barrier((weight_grad, value_grad))
+    weight_grad = weight_grad.astype(F32) * (1.0 / math.sqrt(rows * ctx))
     return (block_out, outer_grad, inner_grad, value_grad, weight_grad)
 
 

time: 209 us -> 167 us (0.80)
  waiting for transfers between devices: 88.3 us -> 41.2 us
  Pallas kernels: 83.3 us -> 89.4 us
    reduce_scatter x1, waiting for transfers between devices: 66.1 us -> 6.09 us  [shards(): lax.psum_scatter(grad_rows, 'ctx', scatter_dimension=0, tiled=True)]
    ppermute x1, waiting for transfers between devices: 0.01 us -> 13 us  [shards(): from_them = lax.ppermute(for_them, 'fsdp', swap)]
    pallas_call x2, Pallas kernels: 43.8 us -> 49.7 us  [prefix(): pl.pallas_call(functools.partial(prefix_kernel, reverse, rows), out_shape...]
  transfers between devices with their start and end apart: 4 -> 4, of which waited for: 2 -> 3; matrix products, arithmetic and copies ran while one was open for 9% -> 10% of each run, Pallas kernels for 22% -> 54%
where the time goes in v3:
time: 167 us; the launch traced here: 166 us
  Pallas kernels  89.4 us (54%)
  waiting for transfers between devices  41.2 us (25%)
  matrix products  15.7 us (9%)
  between operations  14.1 us (8%)
  other arithmetic  3.48 us (2%)
  starting transfers between devices  2.56 us (2%)
    pallas_call x2, Pallas kernels, prefix(): pl.pallas_call(functools.partial(prefix_kernel, reverse, rows), out_shape...  49.7 us
    pallas_call x4, Pallas kernels, by_lanes(): pl.pallas_call(kernel, grid=(channels // LANES,), out_shape=outs, in_spec...  39.7 us
    ppermute x1, waiting for transfers between devices, shards(): other = lax.ppermute(modulated, 'fsdp', swap)  21.4 us
    ppermute x1, waiting for transfers between devices, shards(): from_them = lax.ppermute(for_them, 'fsdp', swap)  13 us
    reduce_scatter x1, waiting for transfers between devices, shards(): lax.psum_scatter(grad_rows, 'ctx', scatter_dimension=0, tiled=True)  6.09 us
    dot_general x1, matrix products, shards(): lax.dot_general(gathered, out_grad, (((0,), (0,)), ((), ())), preferred_e...  4.34 us
    dot_general x1, matrix products, shards(): own = jnp.dot(out_grad, mine.T, preferred_element_type=F32).astype(BF16)  4.16 us
    dot_general x1, matrix products, shards(): jnp.dot(out_grad, theirs.T, preferred_element_type=F32).astype(BF16)  3.85 us
  transfers between devices with their start and end apart: 4, of which 3 were waited for; matrix products, arithmetic and copies ran while one was open for 10% of the time, Pallas kernels for 54%

profile of v3, /device:TPU:0, one launch (start us, length us, event | category | flops | bytes accessed | tf_op | source)
XLA Modules:
  0.0 166.4 jit_solution(8672352664457672058)
XLA Ops:
  7.2 0.0 copy-start
  7.2 0.0 all-gather.2.cloned.1.call-start
  7.2 0.7 all-gather.2.cloned.1.call-update
  7.9 0.0 reduce-scatter.2.cloned.1.call-start
  8.0 7.8 %forward_ends.1 = (f32[16,8,1024]{2,1,0:T(8,128)}, f32[16,1024]{1,0:T(8,128)}) custom-call(bf16[512,1024]{1,0:T(8,128)(2,1)} %inner_ref.5, bf16[512,1024]{1,0:T(8,128)(2,1)} %values_ref.5, f32[16,1024]{1,0:T(8,128)} %bitcast.11), custom_call_target="tpu_custom_call" | custom-call | flops 8388608000 | bytes 2752512 | tf_op jit(solution)/shard_map/forward_ends/pallas_call | solution.py:125
  15.8 25.8 %prefix_ahead.1.incoming_ref = f32[16,1024]{1,0:T(8,128)} custom-call(f32[16,1024]{1,0:T(8,128)} %get-tuple-element.17.end_ref, f32[16,1024]{1,0:T(8,128)} %bitcast.12), custom_call_target="tpu_custom_call" | custom-call | flops 17999998976 | tf_op jit(solution)/shard_map/prefix_ahead/pallas_call | solution.py:174
  41.5 11.5 %forward_finish.1 = (f32[512,1024]{1,0:T(8,128)}, bf16[512,1024]{1,0:T(8,128)(2,1)}) custom-call(bf16[512,1024]{1,0:T(8,128)(2,1)} %inner_ref.5, bf16[512,1024]{1,0:T(8,128)(2,1)} %values_ref.5, bf16[512,1024]{1,0:T(8,128)(2,1)} %outer_ref.5, f32[16,1024]{1,0:T(8,128)} %bitcast.13, f32[16,1024]{1,0:T(8,128)} %bitcast.17, f32[1,1024]{1,0:T(1,128)} %bitcast.19, ...), custom_call_target="tpu_custom_call" | custom-call | flops 12582912000 | bytes 7016448 | tf_op jit(solution)/shard_map/forward_finish/pallas_call | solution.py:125
  53.0 0.8 collective-permute-start
  53.8 21.4 %collective-permute-done = bf16[512,1024]{1,0:T(8,128)(2,1)} collective-permute-done((bf16[512,1024]{1,0:T(8,128)(2,1)}, bf16[512,1024]{1,0:T(8,128)(2,1)}, u32[]{:S(2)}, u32[]{:S(2)}) %collective-permute-start) | collective-permute-done | bytes 1048608 | tf_op jit(solution)/shard_map/ppermute | solution.py:215
  75.2 1.7 %broadcast_select_fusion.1 = (bf16[512,1024]{1,0:T(8,128)(2,1)S(1)}, bf16[512,1024]{1,0:T(8,128)(2,1)S(1)}) fusion(bf16[512,1024]{1,0:T(8,128)(2,1)} %get-tuple-element.18, bf16[512,1024]{1,0:T(8,128)(2,1)} %collective-permute-done, pred[]{:T(512)S(6)} %eq.4), kind=kLoop, calls=%fused_computation.12 | loop fusion | flops 1048576 | bytes 4194305 | tf_op jit(solution)/shard_map/jit(_where)/select_n | solution.py:216
  76.9 0.0 copy-done
  76.9 4.3 %convolution_convert_fusion = bf16[2048,1024]{1,0:T(8,128)(2,1)} fusion(bf16[512,1024]{1,0:T(8,128)(2,1)S(1)} %copy-done, bf16[512,1024]{1,0:T(8,128)(2,1)S(1)} %get-tuple-element.28, bf16[512,1024]{1,0:T(8,128)(2,1)S(1)} %get-tuple-element.27), kind=kOutput, calls=%fused_computation | convolution fusion | flops 2153775104 | bytes 7340032 | tf_op jit(solution)/shard_map/dot_general | solution.py:229
  81.3 0.0 reduce-scatter.2.cloned.1.call-update
  81.3 0.0 all-gather.2.cloned.1.call-done
  81.3 3.9 %fusion.10 = bf16[512,1024]{1,0:T(8,128)(2,1)} fusion(bf16[512,1024]{1,0:T(8,128)(2,1)S(1)} %copy-done, bf16[2048,1024]{1,0:T(8,128)(2,1)} %all-gather.2.cloned.1.call-done, s32[]{:T(128)S(6)} %select_n.22), kind=kOutput, calls=%fused_computation.9 | convolution fusion | flops 1074266112 | bytes 4194308 | tf_op jit(solution)/shard_map/dot_general | solution.py:221
  85.2 1.7 %collective-permute-start.1 = (bf16[512,1024]{1,0:T(8,128)(2,1)}, bf16[512,1024]{1,0:T(8,128)(2,1)}, u32[]{:S(2)}, u32[]{:S(2)}) collective-permute-start(bf16[512,1024]{1,0:T(8,128)(2,1)} %fusion.10), channel_id=1, source_target_pairs={{0,1},{1,0},{2,3},{3,2},{4,5},{5,4},{6,7},{7,6},{8,9},{9,8},{10,11... | collective-permute-start | bytes 3145736 | tf_op jit(solution)/shard_map/ppermute | solution.py:222
  86.9 0.0 copy-start.1
  86.9 4.2 %fusion.13.own_ref = bf16[512,1024]{1,0:T(8,128)(2,1)} fusion(bf16[512,1024]{1,0:T(8,128)(2,1)S(1)} %copy-done, bf16[2048,1024]{1,0:T(8,128)(2,1)} %all-gather.2.cloned.1.call-done, s32[]{:T(128)S(6)} %select_n.21), kind=kOutput, calls=%fused_computation.10 | convolution fusion | flops 1074266112 | bytes 4194308 | tf_op jit(solution)/shard_map/dot_general | solution.py:223
  91.0 0.0 copy-done.1
  91.1 3.3 %convolution_convert_fusion.1 = bf16[512,1024]{1,0:T(8,128)(2,1)} fusion(bf16[2048,1024]{1,0:T(8,128)(2,1)S(1)} %copy-done.1, bf16[512,1024]{1,0:T(8,128)(2,1)S(1)} %get-tuple-element.28, bf16[512,1024]{1,0:T(8,128)(2,1)S(1)} %get-tuple-element.27), kind=kOutput, calls=%fused_computation.8 | convolution fusion | flops 2152202240 | bytes 7340032 | tf_op jit(solution)/shard_map/dot_general | solution.py:233
  94.4 13.0 %collective-permute-done.1.other_ref = bf16[512,1024]{1,0:T(8,128)(2,1)} collective-permute-done((bf16[512,1024]{1,0:T(8,128)(2,1)}, bf16[512,1024]{1,0:T(8,128)(2,1)}, u32[]{:S(2)}, u32[]{:S(2)}) %collective-permute-start.1) | collective-permute-done | bytes 1048608 | tf_op jit(solution)/shard_map/ppermute | solution.py:222
  107.4 8.4 %backward_ends.1 = (f32[16,8,1024]{2,1,0:T(8,128)}, f32[16,1024]{1,0:T(8,128)}) custom-call(bf16[512,1024]{1,0:T(8,128)(2,1)} %fusion.13.own_ref, bf16[512,1024]{1,0:T(8,128)(2,1)} %collective-permute-done.1.other_ref, bf16[512,1024]{1,0:T(8,128)(2,1)} %outer_ref.5, f32[16,1024]{1,0:T(8,128)} %bitcast.14), custom_call_target="tpu_custom_call" | custom-call | flops 8388608000 | bytes 3801088 | tf_op jit(solution)/shard_map/backward_ends/pallas_call | solution.py:125
  115.7 24.0 %prefix_back.1.incoming_ref = f32[16,1024]{1,0:T(8,128)} custom-call(f32[16,1024]{1,0:T(8,128)} %get-tuple-element.21.end_ref, f32[16,1024]{1,0:T(8,128)} %bitcast.15), custom_call_target="tpu_custom_call" | custom-call | flops 17999998976 | tf_op jit(solution)/shard_map/prefix_back/pallas_call | solution.py:174
  139.7 12.0 %backward_finish.1 = (bf16[512,1024]{1,0:T(8,128)(2,1)}, bf16[512,1024]{1,0:T(8,128)(2,1)}, bf16[512,1024]{1,0:T(8,128)(2,1)}) custom-call(bf16[512,1024]{1,0:T(8,128)(2,1)} %fusion.13.own_ref, bf16[512,1024]{1,0:T(8,128)(2,1)} %collective-permute-done.1.other_ref, bf16[512,1024]{1,0:T(8,128)(2,1)} %outer_ref.5, bf16[512,1024]{1,0:T(8,128)(2,1)} %inner_ref.5, ...), custom_call_target="tpu_custom_call" | custom-call | flops 12582912000 | bytes 11210752 | tf_op jit(solution)/shard_map/backward_finish/pallas_call | solution.py:125
  151.7 6.1 %reduce-scatter.2.cloned.1.call-done = bf16[128,1024]{1,0:T(8,128)(2,1)} async-done(((bf16[2048,1024]{1,0:T(8,128)(2,1)}), bf16[128,1024]{1,0:T(8,128)(2,1)}) %reduce-scatter.2.cloned.1.call-update) | async-done | bytes 262160 | tf_op jit(solution)/shard_map/reduce_scatter | solution.py:232
  157.8 1.8 %convert_multiply_fusion = f32[128,1024]{1,0:T(8,128)} fusion(bf16[128,1024]{1,0:T(8,128)(2,1)} %reduce-scatter.2.cloned.1.call-done), kind=kLoop, calls=%fused_computation.13 | loop fusion | flops 262144 | bytes 786432 | tf_op jit(solution)/shard_map/mul | solution.py:246
Async XLA Ops:
  7.2 69.8 %copy-start = (bf16[512,1024]{1,0:T(8,128)(2,1)S(1)}, bf16[512,1024]{1,0:T(8,128)(2,1)}, u32[]{:S(2)}) copy-start(bf16[512,1024]{1,0:T(8,128)(2,1)} %param.15) | copy-start | bytes 3145732
  7.2 74.1 %all-gather.2.cloned.1.call-start = ((), (), s32[]{:S(2)}) async-start(), calls=%async_computation.1 | async-start | bytes 4456448 | tf_op jit(solution)/shard_map/all_gather | solution.py:200
  7.9 149.9 %reduce-scatter.2.cloned.1.call-start = ((), (), s32[]{:S(2)}) async-start(), calls=%async_computation.2 | async-start | bytes 4456448 | tf_op jit(solution)/shard_map/reduce_scatter | solution.py:232
  53.0 22.2 %collective-permute-start = (bf16[512,1024]{1,0:T(8,128)(2,1)}, bf16[512,1024]{1,0:T(8,128)(2,1)}, u32[]{:S(2)}, u32[]{:S(2)}) collective-permute-start(bf16[512,1024]{1,0:T(8,128)(2,1)} %get-tuple-element.18), channel_id=1, source_target_pairs={{0,1},{1,0},{2,3},{3,2},{4,5},{5,4},{6,7},{7,6},{8,9},{9,8},{10,11... | collective-permute-start | bytes 3145736 | tf_op jit(solution)/shard_map/ppermute | solution.py:215
  85.2 22.2 %collective-permute-start.1 = (bf16[512,1024]{1,0:T(8,128)(2,1)}, bf16[512,1024]{1,0:T(8,128)(2,1)}, u32[]{:S(2)}, u32[]{:S(2)}) collective-permute-start(bf16[512,1024]{1,0:T(8,128)(2,1)} %fusion.10), channel_id=1, source_target_pairs={{0,1},{1,0},{2,3},{3,2},{4,5},{5,4},{6,7},{7,6},{8,9},{9,8},{10,11... | collective-permute-start | bytes 3145736 | tf_op jit(solution)/shard_map/ppermute | solution.py:222
  86.9 4.2 %copy-start.1 = (bf16[2048,1024]{1,0:T(8,128)(2,1)S(1)}, bf16[2048,1024]{1,0:T(8,128)(2,1)}, u32[]{:S(2)}) copy-start(bf16[2048,1024]{1,0:T(8,128)(2,1)} %all-gather.2.cloned.1.call-done) | copy-start | bytes 12582916
Sparse Core Ops, SparseCore 0:
  10.2 55.9 all-gather.1
  81.4 76.3 reduce-scatter.1

commit v4 on v3

--- a/solution.py
+++ b/solution.py
@@ -212,6 +212,7 @@
         2,
     )
     if fsdp == 2:
+        grad_swapped = lax.ppermute(out_grad, "fsdp", swap)
         other = lax.ppermute(modulated, "fsdp", swap)
         first = jnp.where(at == 0, modulated, other)
         second = jnp.where(at == 0, other, modulated)
@@ -226,10 +227,29 @@
         partial = jnp.dot(out_grad, panel.T, preferred_element_type=F32).astype(BF16)
         own = lax.psum_scatter(partial, "fsdp", scatter_dimension=1, tiled=True)
         from_them = jnp.zeros_like(own)
-    grad_rows = lax.dot_general(
-        gathered, out_grad, (((0,), (0,)), ((), ())), preferred_element_type=F32
-    ).astype(BF16)
-    weight_grad = lax.psum_scatter(grad_rows, "ctx", scatter_dimension=0, tiled=True)
+    contract = (((0,), (0,)), ((), ()))
+    if fsdp == 2 and ctx % 2 == 0:
+        low = jnp.where(at == 0, out_grad, grad_swapped)
+        high = jnp.where(at == 0, grad_swapped, out_grad)
+        terms = [
+            lax.dot_general(modulated, x, contract, preferred_element_type=F32).astype(BF16)
+            for x in (low, high)
+        ]
+        grad_rows = jnp.concatenate(terms, axis=0)
+        block = lax.psum_scatter(grad_rows, "ctx", scatter_dimension=0, tiled=True)
+        half = ctx // 2
+        route = [
+            ((p * half + k) * 2 + j, (j * half + k) * 2 + p)
+            for p in range(2)
+            for k in range(half)
+            for j in range(2)
+        ]
+        weight_grad = block
+    else:
+        grad_rows = lax.dot_general(
+            gathered, out_grad, contract, preferred_element_type=F32
+        ).astype(BF16)
+        weight_grad = lax.psum_scatter(grad_rows, "ctx", scatter_dimension=0, tiled=True)
     block_out = jnp.dot(gathered, panel, preferred_element_type=F32).astype(BF16)
     pre, end = by_lanes(
         backward_ends, (own, from_them, outer_gate, decay), state_outs, rows, 1
@@ -243,6 +263,8 @@
         2,
     )
     weight_grad, value_grad = lax.optimization_barrier((weight_grad, value_grad))
+    if fsdp == 2 and ctx % 2 == 0:
+        weight_grad = lax.ppermute(weight_grad, ("ctx", "fsdp"), route)
     weight_grad = weight_grad.astype(F32) * (1.0 / math.sqrt(rows * ctx))
     return (block_out, outer_grad, inner_grad, value_grad, weight_grad)
 

time: 167 us -> 169 us (1.012)
  the two profiles are of different devices: /device:TPU:0 before, /device:TPU:3 now
where the time goes in v4:
time: 169 us; the launch traced here: 168 us
  Pallas kernels  84.7 us (50%)
  waiting for transfers between devices  44.2 us (26%)
  matrix products  16.8 us (10%)
  between operations  14.2 us (8%)
  other arithmetic  4.38 us (3%)
  starting transfers between devices  3.66 us (2%)
    pallas_call x2, Pallas kernels, prefix(): pl.pallas_call(functools.partial(prefix_kernel, reverse, rows), out_shape...  45.1 us
    pallas_call x4, Pallas kernels, by_lanes(): pl.pallas_call(kernel, grid=(channels // LANES,), out_shape=outs, in_spec...  39.6 us
    ppermute x1, waiting for transfers between devices, shards(): from_them = lax.ppermute(for_them, 'fsdp', swap)  17.9 us
    all_gather x1, waiting for transfers between devices, shards(): panel = lax.all_gather(out_weight, 'ctx', axis=0, tiled=True)  9.91 us
    ppermute x1, waiting for transfers between devices, shards(): weight_grad = lax.ppermute(weight_grad, ('ctx', 'fsdp'), route)  9.85 us
    ppermute x1, waiting for transfers between devices, shards(): other = lax.ppermute(modulated, 'fsdp', swap)  5.78 us
    dot_general x1, matrix products, shards(): jnp.dot(gathered, panel, preferred_element_type=F32).astype(BF16)  5.49 us
    dot_general x2, matrix products, shards(): lax.dot_general(modulated, x, contract, preferred_element_type=F32)  3.92 us
  transfers between devices with their start and end apart: 6, of which 4 were waited for; matrix products, arithmetic and copies ran while one was open for 12% of the time, Pallas kernels for 50%

profile of v4, /device:TPU:3, one launch (start us, length us, event | category | flops | bytes accessed | tf_op | source)
XLA Modules:
  0.0 168.0 jit_solution(4182882897392056219)
XLA Ops:
  7.2 0.0 all-gather.2.cloned.1.call-start
  7.2 0.7 all-gather.2.cloned.1.call-update
  7.9 0.0 reduce-scatter.2.cloned.1.call-start
  7.9 0.1 collective-permute-start.2
  8.0 7.8 %forward_ends.1 = (f32[16,8,1024]{2,1,0:T(8,128)}, f32[16,1024]{1,0:T(8,128)}) custom-call(bf16[512,1024]{1,0:T(8,128)(2,1)} %inner_ref.5, bf16[512,1024]{1,0:T(8,128)(2,1)} %values_ref.5, f32[16,1024]{1,0:T(8,128)} %bitcast.12), custom_call_target="tpu_custom_call" | custom-call | flops 8388608000 | bytes 2752512 | tf_op jit(solution)/shard_map/forward_ends/pallas_call | solution.py:125
  15.8 20.6 %prefix_ahead.1.incoming_ref = f32[16,1024]{1,0:T(8,128)} custom-call(f32[16,1024]{1,0:T(8,128)} %get-tuple-element.17.end_ref, f32[16,1024]{1,0:T(8,128)} %bitcast.13), custom_call_target="tpu_custom_call" | custom-call | flops 17999998976 | tf_op jit(solution)/shard_map/prefix_ahead/pallas_call | solution.py:174
  36.4 0.0 copy-start.3
  36.4 11.5 %forward_finish.1 = (f32[512,1024]{1,0:T(8,128)}, bf16[512,1024]{1,0:T(8,128)(2,1)}) custom-call(bf16[512,1024]{1,0:T(8,128)(2,1)} %inner_ref.5, bf16[512,1024]{1,0:T(8,128)(2,1)} %values_ref.5, bf16[512,1024]{1,0:T(8,128)(2,1)} %outer_ref.5, f32[16,1024]{1,0:T(8,128)} %bitcast.14, f32[16,1024]{1,0:T(8,128)} %bitcast.18, f32[1,1024]{1,0:T(1,128)} %bitcast.20, ...), custom_call_target="tpu_custom_call" | custom-call | flops 12582912000 | bytes 7016448 | tf_op jit(solution)/shard_map/forward_finish/pallas_call | solution.py:125
  48.0 0.0 copy-start
  48.0 0.0 collective-permute-done.2
  48.0 0.0 copy-done.3
  48.0 2.6 %convolution_convert_fusion = bf16[1024,1024]{1,0:T(8,128)(2,1)S(1)} fusion(bf16[512,1024]{1,0:T(8,128)(2,1)} %get-tuple-element.18, bf16[512,1024]{1,0:T(8,128)(2,1)S(1)} %collective-permute-done.2, bf16[512,1024]{1,0:T(8,128)(2,1)S(1)} %copy-done.3, pred[]{:T(512)S(6)} %eq.2), kind=kOutput, calls=%fused_computation.9 | convolution fusion | flops 1075314688 | bytes 5242881 | tf_op jit(solution)/shard_map/dot_general | solution.py:235
  50.6 0.0 copy-done
  50.6 1.3 convolution_convert_fusion.1
  51.9 2.4 %pad_maximum_fusion = bf16[2048,1024]{1,0:T(8,128)(2,1)} fusion(bf16[1024,1024]{1,0:T(8,128)(2,1)S(1)} %convolution_convert_fusion, bf16[1024,1024]{1,0:T(8,128)(2,1)S(1)} %convolution_convert_fusion.1), kind=kLoop, calls=%fused_computation | loop fusion | flops 8388608 | bytes 8388608 | tf_op jit(solution)/shard_map/concatenate | solution.py:238
  54.4 0.0 reduce-scatter.2.cloned.1.call-update
  54.4 1.3 collective-permute-start
  55.7 9.9 %all-gather.2.cloned.1.call-done = bf16[2048,1024]{1,0:T(8,128)(2,1)} async-done(((bf16[128,1024]{1,0:T(8,128)(2,1)}), bf16[2048,1024]{1,0:T(8,128)(2,1)}) %all-gather.2.cloned.1.call-update) | async-done | bytes 4194320 | tf_op jit(solution)/shard_map/all_gather | solution.py:200
  65.6 3.8 %fusion.17 = bf16[512,1024]{1,0:T(8,128)(2,1)} fusion(bf16[512,1024]{1,0:T(8,128)(2,1)S(1)} %copy-done.3, bf16[2048,1024]{1,0:T(8,128)(2,1)} %all-gather.2.cloned.1.call-done, s32[]{:T(128)S(6)} %select_n.30), kind=kOutput, calls=%fused_computation.14 | convolution fusion | flops 1074266112 | bytes 4194308 | tf_op jit(solution)/shard_map/dot_general | solution.py:222
  69.5 0.3 collective-permute-start.1
  69.7 0.0 copy-start.2
  69.7 5.8 %collective-permute-done = bf16[512,1024]{1,0:T(8,128)(2,1)S(1)} collective-permute-done((bf16[512,1024]{1,0:T(8,128)(2,1)S(1)}, bf16[512,1024]{1,0:T(8,128)(2,1)S(1)}, u32[]{:S(2)}, u32[]{:S(2)}) %collective-permute-start) | collective-permute-done | bytes 1048608 | tf_op jit(solution)/shard_map/ppermute | solution.py:216
  75.5 1.1 broadcast_select_fusion.1
  76.6 0.0 copy-done.2
  76.6 3.6 %fusion.20.own_ref = bf16[512,1024]{1,0:T(8,128)(2,1)} fusion(bf16[512,1024]{1,0:T(8,128)(2,1)} %param.15, bf16[2048,1024]{1,0:T(8,128)(2,1)S(1)} %copy-done.2, s32[]{:T(128)S(6)} %select_n.29), kind=kOutput, calls=%fused_computation.15 | convolution fusion | flops 1074266112 | bytes 4194308 | tf_op jit(solution)/shard_map/dot_general | solution.py:224
  80.2 17.9 %collective-permute-done.1.other_ref = bf16[512,1024]{1,0:T(8,128)(2,1)} collective-permute-done((bf16[512,1024]{1,0:T(8,128)(2,1)}, bf16[512,1024]{1,0:T(8,128)(2,1)}, u32[]{:S(2)}, u32[]{:S(2)}) %collective-permute-start.1) | collective-permute-done | bytes 1048608 | tf_op jit(solution)/shard_map/ppermute | solution.py:223
  98.1 8.3 %backward_ends.1 = (f32[16,8,1024]{2,1,0:T(8,128)}, f32[16,1024]{1,0:T(8,128)}) custom-call(bf16[512,1024]{1,0:T(8,128)(2,1)} %fusion.20.own_ref, bf16[512,1024]{1,0:T(8,128)(2,1)} %collective-permute-done.1.other_ref, bf16[512,1024]{1,0:T(8,128)(2,1)} %outer_ref.5, f32[16,1024]{1,0:T(8,128)} %bitcast.15), custom_call_target="tpu_custom_call" | custom-call | flops 8388608000 | bytes 3801088 | tf_op jit(solution)/shard_map/backward_ends/pallas_call | solution.py:125
  106.4 24.5 %prefix_back.1.incoming_ref = f32[16,1024]{1,0:T(8,128)} custom-call(f32[16,1024]{1,0:T(8,128)} %get-tuple-element.21.end_ref, f32[16,1024]{1,0:T(8,128)} %bitcast.16), custom_call_target="tpu_custom_call" | custom-call | flops 17999998976 | tf_op jit(solution)/shard_map/prefix_back/pallas_call | solution.py:174
  130.9 0.0 copy-start.1
  130.9 12.0 %backward_finish.1 = (bf16[512,1024]{1,0:T(8,128)(2,1)}, bf16[512,1024]{1,0:T(8,128)(2,1)}, bf16[512,1024]{1,0:T(8,128)(2,1)}) custom-call(bf16[512,1024]{1,0:T(8,128)(2,1)} %fusion.20.own_ref, bf16[512,1024]{1,0:T(8,128)(2,1)} %collective-permute-done.1.other_ref, bf16[512,1024]{1,0:T(8,128)(2,1)} %outer_ref.5, bf16[512,1024]{1,0:T(8,128)(2,1)} %inner_ref.5, ...), custom_call_target="tpu_custom_call" | custom-call | flops 12582912000 | bytes 11210752 | tf_op jit(solution)/shard_map/backward_finish/pallas_call | solution.py:125
  143.0 0.0 reduce-scatter.2.cloned.1.call-done
  143.0 1.9 %collective-permute-start.3 = (bf16[128,1024]{1,0:T(8,128)(2,1)}, bf16[128,1024]{1,0:T(8,128)(2,1)S(1)}, u32[]{:S(2)}, u32[]{:S(2)}) collective-permute-start(bf16[128,1024]{1,0:T(8,128)(2,1)} %reduce-scatter.2.cloned.1.call-done), channel_id=1, source_target_pairs={{0,0},{1,16},{2,2},{3,18},{4,4},{5,20},{6,6},{7,22},{8,8},{9,24},{... | collective-permute-start | bytes 786440 | tf_op jit(solution)/shard_map/ppermute | solution.py:267
  144.9 0.0 copy-done.1
  144.9 5.5 %fusion.8 = bf16[512,1024]{1,0:T(8,128)(2,1)} fusion(bf16[2048,1024]{1,0:T(8,128)(2,1)} %all-gather.2.cloned.1.call-done, bf16[512,1024]{1,0:T(8,128)(2,1)S(1)} %copy-done.1, bf16[512,1024]{1,0:T(8,128)(2,1)S(1)} %get-tuple-element.27), kind=kOutput, calls=%fused_computation.11 | convolution fusion | flops 2152202240 | bytes 7340032 | tf_op jit(solution)/shard_map/dot_general | solution.py:253
  150.4 9.9 %collective-permute-done.3 = bf16[128,1024]{1,0:T(8,128)(2,1)S(1)} collective-permute-done((bf16[128,1024]{1,0:T(8,128)(2,1)}, bf16[128,1024]{1,0:T(8,128)(2,1)S(1)}, u32[]{:S(2)}, u32[]{:S(2)}) %collective-permute-start.3) | collective-permute-done | bytes 262176 | tf_op jit(solution)/shard_map/ppermute | solution.py:267
  160.3 0.9 convert_multiply_fusion
Async XLA Ops:
  7.2 58.4 %all-gather.2.cloned.1.call-start = ((), (), s32[]{:S(2)}) async-start(), calls=%async_computation.1 | async-start | bytes 4456448 | tf_op jit(solution)/shard_map/all_gather | solution.py:200
  7.9 135.1 %reduce-scatter.2.cloned.1.call-start = ((), (), s32[]{:S(2)}) async-start(), calls=%async_computation.2 | async-start | bytes 4456448 | tf_op jit(solution)/shard_map/reduce_scatter | solution.py:239
  7.9 40.0 %collective-permute-start.2 = (bf16[512,1024]{1,0:T(8,128)(2,1)}, bf16[512,1024]{1,0:T(8,128)(2,1)S(1)}, u32[]{:S(2)}, u32[]{:S(2)}) collective-permute-start(bf16[512,1024]{1,0:T(8,128)(2,1)} %param.15), channel_id=1, source_target_pairs={{0,1},{1,0},{2,3},{3,2},{4,5},{5,4},{6,7},{7,6},{8,9},{9,8},{10,11... | collective-permute-start | bytes 3145736 | tf_op jit(solution)/shard_map/ppermute | solution.py:215
  36.4 11.6 %copy-start.3 = (bf16[512,1024]{1,0:T(8,128)(2,1)S(1)}, bf16[512,1024]{1,0:T(8,128)(2,1)}, u32[]{:S(2)}) copy-start(bf16[512,1024]{1,0:T(8,128)(2,1)} %param.15) | copy-start | bytes 3145732
  48.0 2.6 %copy-start = (bf16[512,1024]{1,0:T(8,128)(2,1)S(1)}, bf16[512,1024]{1,0:T(8,128)(2,1)}, u32[]{:S(2)}) copy-start(bf16[512,1024]{1,0:T(8,128)(2,1)} %get-tuple-element.18) | copy-start | bytes 3145732
  54.4 21.1 %collective-permute-start = (bf16[512,1024]{1,0:T(8,128)(2,1)S(1)}, bf16[512,1024]{1,0:T(8,128)(2,1)S(1)}, u32[]{:S(2)}, u32[]{:S(2)}) collective-permute-start(bf16[512,1024]{1,0:T(8,128)(2,1)S(1)} %copy-done), channel_id=1, source_target_pairs={{0,1},{1,0},{2,3},{3,2},{4,5},{5,4},{6,7},{7,6},{8,9},{9,8},{10,11... | collective-permute-start | bytes 3145736 | tf_op jit(solution)/shard_map/ppermute | solution.py:216
  69.5 28.6 %collective-permute-start.1 = (bf16[512,1024]{1,0:T(8,128)(2,1)}, bf16[512,1024]{1,0:T(8,128)(2,1)}, u32[]{:S(2)}, u32[]{:S(2)}) collective-permute-start(bf16[512,1024]{1,0:T(8,128)(2,1)} %fusion.17), channel_id=1, source_target_pairs={{0,1},{1,0},{2,3},{3,2},{4,5},{5,4},{6,7},{7,6},{8,9},{9,8},{10,11... | collective-permute-start | bytes 3145736 | tf_op jit(solution)/shard_map/ppermute | solution.py:223
  69.7 6.9 %copy-start.2 = (bf16[2048,1024]{1,0:T(8,128)(2,1)S(1)}, bf16[2048,1024]{1,0:T(8,128)(2,1)}, u32[]{:S(2)}) copy-start(bf16[2048,1024]{1,0:T(8,128)(2,1)} %all-gather.2.cloned.1.call-done) | copy-start | bytes 12582916
  130.9 14.0 %copy-start.1 = (bf16[512,1024]{1,0:T(8,128)(2,1)S(1)}, bf16[512,1024]{1,0:T(8,128)(2,1)}, u32[]{:S(2)}) copy-start(bf16[512,1024]{1,0:T(8,128)(2,1)} %get-tuple-element.28) | copy-start | bytes 3145732
  143.0 17.3 %collective-permute-start.3 = (bf16[128,1024]{1,0:T(8,128)(2,1)}, bf16[128,1024]{1,0:T(8,128)(2,1)S(1)}, u32[]{:S(2)}, u32[]{:S(2)}) collective-permute-start(bf16[128,1024]{1,0:T(8,128)(2,1)} %reduce-scatter.2.cloned.1.call-done), channel_id=1, source_target_pairs={{0,0},{1,16},{2,2},{3,18},{4,4},{5,20},{6,6},{7,22},{8,8},{9,24},{... | collective-permute-start | bytes 786440 | tf_op jit(solution)/shard_map/ppermute | solution.py:267
Sparse Core Ops, SparseCore 0:
  10.2 55.3 all-gather.1
  69.5 70.7 reduce-scatter.1

commit v5 on v3

--- a/solution.py
+++ b/solution.py
@@ -148,7 +148,7 @@
     upto = end_ref[...]
     before = jnp.zeros_like(upto)
     for k, hop in enumerate(hops):
-        sent[k] = upto
+        sent[k] = upto.astype(BF16)
         copy = pltpu.make_async_remote_copy(
             src_ref=sent.at[k],
             dst_ref=got.at[k],
@@ -162,7 +162,7 @@
         far = jnp.exp(-decay * float(rows * hop))
         copy.wait()
         inside = (me + hop < n) if reverse else (me >= hop)
-        term = got[k] * jnp.where(inside, 1.0, 0.0)
+        term = got[k].astype(F32) * jnp.where(inside, 1.0, 0.0)
         before = before + near * term
         upto = upto + far * term
     out_ref[...] = before
@@ -177,8 +177,8 @@
         in_specs=[whole, whole],
         out_specs=whole,
         scratch_shapes=[
-            pltpu.VMEM((hops,) + end.shape, F32),
-            pltpu.VMEM((hops,) + end.shape, F32),
+            pltpu.VMEM((hops,) + end.shape, BF16),
+            pltpu.VMEM((hops,) + end.shape, BF16),
             pltpu.SemaphoreType.DMA((hops,)),
             pltpu.SemaphoreType.DMA((hops,)),
         ],

time: 167 us -> 163 us (0.976)
  Pallas kernels: 89.4 us -> 79.5 us
  waiting for transfers between devices: 41.2 us -> 45.5 us
    pallas_call x2, Pallas kernels: 49.7 us -> 40 us  [prefix(): pl.pallas_call(functools.partial(prefix_kernel, reverse, rows), out_shape...]
    reduce_scatter x1, waiting for transfers between devices: 6.09 us -> 9.76 us  [shards(): lax.psum_scatter(grad_rows, 'ctx', scatter_dimension=0, tiled=True)]
  transfers between devices with their start and end apart: 4 -> 4, of which waited for: 3 -> 3; matrix products, arithmetic and copies ran while one was open for 10% -> 11% of each run, Pallas kernels for 54% -> 49%
where the time goes in v5:
time: 163 us; the launch traced here: 162 us
  Pallas kernels  79.5 us (49%)
  waiting for transfers between devices  45.5 us (28%)
  matrix products  15.7 us (10%)
  between operations  14.1 us (9%)
  other arithmetic  3.48 us (2%)
  starting transfers between devices  3.28 us (2%)
    pallas_call x2, Pallas kernels, prefix(): pl.pallas_call(functools.partial(prefix_kernel, reverse, rows), out_shape...  40 us
    pallas_call x4, Pallas kernels, by_lanes(): pl.pallas_call(kernel, grid=(channels // LANES,), out_shape=outs, in_spec...  39.5 us
    ppermute x1, waiting for transfers between devices, shards(): other = lax.ppermute(modulated, 'fsdp', swap)  21.6 us
    ppermute x1, waiting for transfers between devices, shards(): from_them = lax.ppermute(for_them, 'fsdp', swap)  13.4 us
    reduce_scatter x1, waiting for transfers between devices, shards(): lax.psum_scatter(grad_rows, 'ctx', scatter_dimension=0, tiled=True)  9.76 us
    dot_general x1, matrix products, shards(): lax.dot_general(gathered, out_grad, (((0,), (0,)), ((), ())), preferred_e...  4.34 us
    dot_general x1, matrix products, shards(): own = jnp.dot(out_grad, mine.T, preferred_element_type=F32).astype(BF16)  4.12 us
    dot_general x1, matrix products, shards(): jnp.dot(out_grad, theirs.T, preferred_element_type=F32).astype(BF16)  3.86 us
  transfers between devices with their start and end apart: 4, of which 3 were waited for; matrix products, arithmetic and copies ran while one was open for 11% of the time, Pallas kernels for 49%

profile of v5, /device:TPU:0, one launch (start us, length us, event | category | flops | bytes accessed | tf_op | source)
XLA Modules:
  0.0 161.5 jit_solution(12565451199381101544)
XLA Ops:
  7.2 0.0 copy-start
  7.2 0.0 all-gather.2.cloned.1.call-start
  7.2 0.7 all-gather.2.cloned.1.call-update
  7.9 0.0 reduce-scatter.2.cloned.1.call-start
  8.0 7.8 %forward_ends.1 = (f32[16,8,1024]{2,1,0:T(8,128)}, f32[16,1024]{1,0:T(8,128)}) custom-call(bf16[512,1024]{1,0:T(8,128)(2,1)} %inner_ref.5, bf16[512,1024]{1,0:T(8,128)(2,1)} %values_ref.5, f32[16,1024]{1,0:T(8,128)} %bitcast.11), custom_call_target="tpu_custom_call" | custom-call | flops 8388608000 | bytes 2752512 | tf_op jit(solution)/shard_map/forward_ends/pallas_call | solution.py:125
  15.8 21.5 %prefix_ahead.1.incoming_ref = f32[16,1024]{1,0:T(8,128)} custom-call(f32[16,1024]{1,0:T(8,128)} %get-tuple-element.17.end_ref, f32[16,1024]{1,0:T(8,128)} %bitcast.12), custom_call_target="tpu_custom_call" | custom-call | flops 17999998976 | tf_op jit(solution)/shard_map/prefix_ahead/pallas_call | solution.py:174
  37.2 11.3 %forward_finish.1 = (f32[512,1024]{1,0:T(8,128)}, bf16[512,1024]{1,0:T(8,128)(2,1)}) custom-call(bf16[512,1024]{1,0:T(8,128)(2,1)} %inner_ref.5, bf16[512,1024]{1,0:T(8,128)(2,1)} %values_ref.5, bf16[512,1024]{1,0:T(8,128)(2,1)} %outer_ref.5, f32[16,1024]{1,0:T(8,128)} %bitcast.13, f32[16,1024]{1,0:T(8,128)} %bitcast.17, f32[1,1024]{1,0:T(1,128)} %bitcast.19, ...), custom_call_target="tpu_custom_call" | custom-call | flops 12582912000 | bytes 7016448 | tf_op jit(solution)/shard_map/forward_finish/pallas_call | solution.py:125
  48.5 1.7 %collective-permute-start = (bf16[512,1024]{1,0:T(8,128)(2,1)}, bf16[512,1024]{1,0:T(8,128)(2,1)}, u32[]{:S(2)}, u32[]{:S(2)}) collective-permute-start(bf16[512,1024]{1,0:T(8,128)(2,1)} %get-tuple-element.18), channel_id=1, source_target_pairs={{0,1},{1,0},{2,3},{3,2},{4,5},{5,4},{6,7},{7,6},{8,9},{9,8},{10,11... | collective-permute-start | bytes 3145736 | tf_op jit(solution)/shard_map/ppermute | solution.py:215
  50.2 21.6 %collective-permute-done = bf16[512,1024]{1,0:T(8,128)(2,1)} collective-permute-done((bf16[512,1024]{1,0:T(8,128)(2,1)}, bf16[512,1024]{1,0:T(8,128)(2,1)}, u32[]{:S(2)}, u32[]{:S(2)}) %collective-permute-start) | collective-permute-done | bytes 1048608 | tf_op jit(solution)/shard_map/ppermute | solution.py:215
  71.8 1.7 %broadcast_select_fusion.1 = (bf16[512,1024]{1,0:T(8,128)(2,1)S(1)}, bf16[512,1024]{1,0:T(8,128)(2,1)S(1)}) fusion(bf16[512,1024]{1,0:T(8,128)(2,1)} %get-tuple-element.18, bf16[512,1024]{1,0:T(8,128)(2,1)} %collective-permute-done, pred[]{:T(512)S(6)} %eq.4), kind=kLoop, calls=%fused_computation.12 | loop fusion | flops 1048576 | bytes 4194305 | tf_op jit(solution)/shard_map/jit(_where)/select_n | solution.py:216
  73.5 0.0 copy-done
  73.5 4.3 %convolution_convert_fusion = bf16[2048,1024]{1,0:T(8,128)(2,1)} fusion(bf16[512,1024]{1,0:T(8,128)(2,1)S(1)} %copy-done, bf16[512,1024]{1,0:T(8,128)(2,1)S(1)} %get-tuple-element.28, bf16[512,1024]{1,0:T(8,128)(2,1)S(1)} %get-tuple-element.27), kind=kOutput, calls=%fused_computation | convolution fusion | flops 2153775104 | bytes 7340032 | tf_op jit(solution)/shard_map/dot_general | solution.py:229
  77.9 0.0 reduce-scatter.2.cloned.1.call-update
  77.9 0.0 all-gather.2.cloned.1.call-done
  77.9 3.9 %fusion.10 = bf16[512,1024]{1,0:T(8,128)(2,1)} fusion(bf16[512,1024]{1,0:T(8,128)(2,1)S(1)} %copy-done, bf16[2048,1024]{1,0:T(8,128)(2,1)} %all-gather.2.cloned.1.call-done, s32[]{:T(128)S(6)} %select_n.22), kind=kOutput, calls=%fused_computation.9 | convolution fusion | flops 1074266112 | bytes 4194308 | tf_op jit(solution)/shard_map/dot_general | solution.py:221
  81.8 1.5 collective-permute-start.1
  83.2 0.0 copy-start.1
  83.2 4.1 %fusion.13.own_ref = bf16[512,1024]{1,0:T(8,128)(2,1)} fusion(bf16[512,1024]{1,0:T(8,128)(2,1)S(1)} %copy-done, bf16[2048,1024]{1,0:T(8,128)(2,1)} %all-gather.2.cloned.1.call-done, s32[]{:T(128)S(6)} %select_n.21), kind=kOutput, calls=%fused_computation.10 | convolution fusion | flops 1074266112 | bytes 4194308 | tf_op jit(solution)/shard_map/dot_general | solution.py:223
  87.4 0.0 copy-done.1
  87.4 3.3 %convolution_convert_fusion.1 = bf16[512,1024]{1,0:T(8,128)(2,1)} fusion(bf16[2048,1024]{1,0:T(8,128)(2,1)S(1)} %copy-done.1, bf16[512,1024]{1,0:T(8,128)(2,1)S(1)} %get-tuple-element.28, bf16[512,1024]{1,0:T(8,128)(2,1)S(1)} %get-tuple-element.27), kind=kOutput, calls=%fused_computation.8 | convolution fusion | flops 2152202240 | bytes 7340032 | tf_op jit(solution)/shard_map/dot_general | solution.py:233
  90.7 13.4 %collective-permute-done.1.other_ref = bf16[512,1024]{1,0:T(8,128)(2,1)} collective-permute-done((bf16[512,1024]{1,0:T(8,128)(2,1)}, bf16[512,1024]{1,0:T(8,128)(2,1)}, u32[]{:S(2)}, u32[]{:S(2)}) %collective-permute-start.1) | collective-permute-done | bytes 1048608 | tf_op jit(solution)/shard_map/ppermute | solution.py:222
  104.1 8.4 %backward_ends.1 = (f32[16,8,1024]{2,1,0:T(8,128)}, f32[16,1024]{1,0:T(8,128)}) custom-call(bf16[512,1024]{1,0:T(8,128)(2,1)} %fusion.13.own_ref, bf16[512,1024]{1,0:T(8,128)(2,1)} %collective-permute-done.1.other_ref, bf16[512,1024]{1,0:T(8,128)(2,1)} %outer_ref.5, f32[16,1024]{1,0:T(8,128)} %bitcast.14), custom_call_target="tpu_custom_call" | custom-call | flops 8388608000 | bytes 3801088 | tf_op jit(solution)/shard_map/backward_ends/pallas_call | solution.py:125
  112.5 18.5 %prefix_back.1.incoming_ref = f32[16,1024]{1,0:T(8,128)} custom-call(f32[16,1024]{1,0:T(8,128)} %get-tuple-element.21.end_ref, f32[16,1024]{1,0:T(8,128)} %bitcast.15), custom_call_target="tpu_custom_call" | custom-call | flops 17999998976 | tf_op jit(solution)/shard_map/prefix_back/pallas_call | solution.py:174
  131.1 12.1 %backward_finish.1 = (bf16[512,1024]{1,0:T(8,128)(2,1)}, bf16[512,1024]{1,0:T(8,128)(2,1)}, bf16[512,1024]{1,0:T(8,128)(2,1)}) custom-call(bf16[512,1024]{1,0:T(8,128)(2,1)} %fusion.13.own_ref, bf16[512,1024]{1,0:T(8,128)(2,1)} %collective-permute-done.1.other_ref, bf16[512,1024]{1,0:T(8,128)(2,1)} %outer_ref.5, bf16[512,1024]{1,0:T(8,128)(2,1)} %inner_ref.5, ...), custom_call_target="tpu_custom_call" | custom-call | flops 12582912000 | bytes 11210752 | tf_op jit(solution)/shard_map/backward_finish/pallas_call | solution.py:125
  143.1 9.8 %reduce-scatter.2.cloned.1.call-done = bf16[128,1024]{1,0:T(8,128)(2,1)} async-done(((bf16[2048,1024]{1,0:T(8,128)(2,1)}), bf16[128,1024]{1,0:T(8,128)(2,1)}) %reduce-scatter.2.cloned.1.call-update) | async-done | bytes 262160 | tf_op jit(solution)/shard_map/reduce_scatter | solution.py:232
  152.9 1.8 %convert_multiply_fusion = f32[128,1024]{1,0:T(8,128)} fusion(bf16[128,1024]{1,0:T(8,128)(2,1)} %reduce-scatter.2.cloned.1.call-done), kind=kLoop, calls=%fused_computation.13 | loop fusion | flops 262144 | bytes 786432 | tf_op jit(solution)/shard_map/mul | solution.py:246
Async XLA Ops:
  7.2 66.3 %copy-start = (bf16[512,1024]{1,0:T(8,128)(2,1)S(1)}, bf16[512,1024]{1,0:T(8,128)(2,1)}, u32[]{:S(2)}) copy-start(bf16[512,1024]{1,0:T(8,128)(2,1)} %param.15) | copy-start | bytes 3145732
  7.2 70.7 %all-gather.2.cloned.1.call-start = ((), (), s32[]{:S(2)}) async-start(), calls=%async_computation.1 | async-start | bytes 4456448 | tf_op jit(solution)/shard_map/all_gather | solution.py:200
  7.9 145.0 %reduce-scatter.2.cloned.1.call-start = ((), (), s32[]{:S(2)}) async-start(), calls=%async_computation.2 | async-start | bytes 4456448 | tf_op jit(solution)/shard_map/reduce_scatter | solution.py:232
  48.5 23.3 %collective-permute-start = (bf16[512,1024]{1,0:T(8,128)(2,1)}, bf16[512,1024]{1,0:T(8,128)(2,1)}, u32[]{:S(2)}, u32[]{:S(2)}) collective-permute-start(bf16[512,1024]{1,0:T(8,128)(2,1)} %get-tuple-element.18), channel_id=1, source_target_pairs={{0,1},{1,0},{2,3},{3,2},{4,5},{5,4},{6,7},{7,6},{8,9},{9,8},{10,11... | collective-permute-start | bytes 3145736 | tf_op jit(solution)/shard_map/ppermute | solution.py:215
  81.8 22.3 %collective-permute-start.1 = (bf16[512,1024]{1,0:T(8,128)(2,1)}, bf16[512,1024]{1,0:T(8,128)(2,1)}, u32[]{:S(2)}, u32[]{:S(2)}) collective-permute-start(bf16[512,1024]{1,0:T(8,128)(2,1)} %fusion.10), channel_id=1, source_target_pairs={{0,1},{1,0},{2,3},{3,2},{4,5},{5,4},{6,7},{7,6},{8,9},{9,8},{10,11... | collective-permute-start | bytes 3145736 | tf_op jit(solution)/shard_map/ppermute | solution.py:222
  83.2 4.1 %copy-start.1 = (bf16[2048,1024]{1,0:T(8,128)(2,1)S(1)}, bf16[2048,1024]{1,0:T(8,128)(2,1)}, u32[]{:S(2)}) copy-start(bf16[2048,1024]{1,0:T(8,128)(2,1)} %all-gather.2.cloned.1.call-done) | copy-start | bytes 12582916
Sparse Core Ops, SparseCore 0:
  10.2 54.7 all-gather.1
  78.0 74.8 reduce-scatter.1
